TPU v7x, 1024 devices: a whole 8x8x8 slice. The times are simulated.
1024 devices in a mesh: dom: 64 (over x, z), sub: 16 (over y, core).
Axes of the slice: x: 8, y: 8, z: 8, core: 2. Of those that a mesh axis runs over, the one named last changes fastest.
Arguments:
- a_blocks: bfloat16 [64, 768, 8, 64, 64], P('dom', 'sub'), may hold values from -0.25 to 0.25
- p_blocks: bfloat16 [64, 768, 64, 64], P('dom', 'sub'), may hold values from -2.09375 to 2.09375
- a_cols: int32 [64, 768, 8], P('dom', 'sub'), may hold values from 0 to 143
- tile_of_item: int32 [64, 768, 8], P('dom', 'sub'), may hold values from 0 to 191, as said below
Outputs:
- coarse: bfloat16 [64, 192, 64, 64], P('dom')
Inputs may be any that keep to these rules, and one draw needn't show every extreme that they name: `tile_of_item`: within one partition, the blocks held by one device name at most 8 distinct tiles of each sub index, and exactly 8 of some sub index.
All inputs are finite; a program needn't handle non-finite values.
Results may differ from a plain program's by a relative error of at most 0.0049.
Values may be sent and summed in bfloat16 or wider, within the bound.
No kernel may reach another device: no remote copies, remote signals or barrier semaphores. Data moves between devices by JAX's collectives and lax.ppermute only.
A program may use at most 64 MiB of HBM per device.

v0:
```python
import math

import jax
import jax.numpy as jnp
from jax import lax
from jax.sharding import PartitionSpec as P

CAP = 8
CB = 2
KC = 6


def padded(x, sides, width):
    for axis, dim in sides:
        devices, length = (lax.axis_size(axis), x.shape[dim])
        up = [(i, (i + 1) % devices) for i in range(devices - 1)]
        down = [(j, i) for i, j in up]
        last = lax.slice_in_dim(x, length - width, length, axis=dim)
        leading = lax.slice_in_dim(x, 0, width, axis=dim)
        before = lax.ppermute(last, axis, up)
        after = lax.ppermute(leading, axis, down)
        x = jnp.concatenate([before, x, after], axis=dim)
    return x


def accumulate(blocks, own_rows, ghosts, cols, targets, segments):
    fine_rows, per_row, width = (blocks.shape[0], blocks.shape[1], blocks.shape[2])
    step_rows = math.gcd(fine_rows, 16)

    def one_step(turn, total):
        start = turn * step_rows
        block_part = lax.dynamic_slice_in_dim(blocks, start, step_rows, 0)
        row_part = lax.dynamic_slice_in_dim(own_rows, start, step_rows, 0)
        col_part = lax.dynamic_slice_in_dim(cols, start, step_rows, 0).reshape(-1)
        target_part = lax.dynamic_slice_in_dim(targets, start, step_rows, 0).reshape(-1)
        ghost = jnp.take(ghosts, col_part, axis=0).reshape(step_rows, per_row, width, width)
        product = jnp.einsum(
            "ikab,ikbc->ikac", block_part, ghost, preferred_element_type=jnp.float32
        ).astype(jnp.bfloat16)
        terms = jnp.einsum("iba,ikbc->ikac", row_part, product, preferred_element_type=jnp.float32)
        return total + jax.ops.segment_sum(terms.reshape(-1, width, width), target_part, segments)

    start_total = jnp.zeros((segments, width, width), jnp.float32)
    return lax.fori_loop(0, fine_rows // step_rows, one_step, start_total)


def body(a_blocks, p_blocks, a_cols, tile_of_item):
    blocks = a_blocks[0]
    own_rows = p_blocks[0]
    cols = a_cols[0]
    tiles = tile_of_item[0]
    fine_rows, per_row, width = (blocks.shape[0], blocks.shape[1], blocks.shape[2])
    ghosts = padded(p_blocks, (("dom", 0),), 1).reshape(3 * fine_rows, width, width)
    peers = lax.axis_size("sub")
    mine_index = lax.axis_index("sub")
    own = CB * KC
    group = peers * own
    flat_tiles = tiles.reshape(-1)
    counts = jax.ops.segment_sum(jnp.ones_like(flat_tiles), flat_tiles, group)
    present = (counts > 0).astype(jnp.int32).reshape(peers, own)
    ranks = jnp.cumsum(present, axis=1) - 1
    peer_ids = jnp.arange(peers, dtype=jnp.int32)[:, None]
    table = jnp.where(present > 0, peer_ids * CAP + ranks, peers * CAP).reshape(-1)
    matches = flat_tiles[:, None] == jnp.arange(group, dtype=jnp.int32)[None, :]
    item_slot = jnp.sum(jnp.where(matches, table[None, :], 0), axis=1).reshape(fine_rows, per_row)
    slot_tile = jax.ops.segment_max(jnp.arange(group, dtype=jnp.int32), table, peers * CAP + 1)[
        : peers * CAP
    ]
    slot_tile = jnp.where(slot_tile < 0, -1, slot_tile).reshape(peers, CAP)
    slots = accumulate(blocks, own_rows, ghosts, cols, item_slot, peers * CAP + 1)[: peers * CAP]
    slots = slots.reshape(peers, CAP, width, width)
    received, received_ids = (
        lax.all_to_all(slots, "sub", split_axis=0, concat_axis=0, tiled=True),
        lax.all_to_all(slot_tile, "sub", split_axis=0, concat_axis=0, tiled=True),
    )
    flat_ids = received_ids.reshape(-1)
    local_ids = jnp.where(flat_ids >= 0, flat_ids - mine_index * own, own)
    mine = jax.ops.segment_sum(received.reshape(-1, width, width), local_ids, own + 1)[:own]
    finished = mine.astype(jnp.bfloat16)
    gathered = lax.all_gather(finished, "sub", axis=0, tiled=True)
    return gathered[None]


def solution(mesh):
    placed = (
        P("dom", "sub", None, None, None),
        P("dom", "sub", None, None),
        P("dom", "sub", None),
        P("dom", "sub", None),
    )
    return jax.shard_map(
        body, mesh=mesh, in_specs=placed, out_specs=P("dom", None, None, None), check_vma=False
    )
```

profile of v0, /device:TPU:1, one launch (start us, length us, event | category | flops | bytes accessed | tf_op | source)
XLA Modules:
  0.0 299.0 jit_solution(17162667578119344867)
XLA Ops:
  6.5 5.8 %collective-permute-start = (bf16[1,48,64,64]{3,2,1,0:T(8,128)(2,1)}, bf16[1,48,64,64]{3,2,1,0:T(8,128)(2,1)S(1)}, u32[]{:S(2)}, u32[]{:S(2)}) collective-permute-start(bf16[1,48,64,64]{3,2,1,0:T(8,128)(2,1)} %param.7), channel_id=1, source_target_pairs={{0,16},{16,32},{32,48},{48,64},{64,80},{80,96},{96,112},{112,128},... | collective-permute-start | bytes 1179656 | tf_op jit(solution)/shard_map/ppermute | solution.py:20
  12.3 1.3 collective-permute-start.1
  13.6 0.8 copy.22
  14.4 0.1 reshape.189
  14.5 3.9 %scatter_custom_fusion.1 = s32[192]{0:T(256)S(1)} fusion(s32[384]{0:T(512)S(1)} %reshape.189, s32[384]{0:T(512)S(1)} %broadcast.136, s32[]{:T(128)} %constant.82.clone.1), kind=kCustom, calls=%fused_computation.33 | custom fusion | flops 384 | bytes 772 | tf_op jit(solution)/shard_map/scatter-add | solution.py:59
  18.5 0.2 reduce_window_sum.11
  18.7 0.1 add.89
  18.8 1.9 scatter_custom_fusion.2
  20.8 0.6 compare_select_fusion.2
  21.4 12.9 %all-to-all-start = ((s32[16,1,8]{2,1,0:T(1,128)}), s32[16,1,8]{2,1,0:T(1,128)S(1)}, u32[]{:S(2)}, u32[]{:S(2)}) async-start(s32[16,1,8]{2,1,0:T(1,128)} %bitcast.6), calls=%async_computation | async-start | bytes 16384 | tf_op jit(solution)/shard_map/all_to_all | solution.py:74
  34.4 0.1 select_reduce_fusion
  34.5 0.1 reshape.167
  34.6 0.8 copy.26
  35.3 3.1 %pad_maximum_fusion = bf16[3,48,64,64]{3,2,1,0:T(8,128)(2,1)} fusion(bf16[1,48,64,64]{3,2,1,0:T(8,128)(2,1)S(1)} %collective-permute-done.1, bf16[1,48,64,64]{3,2,1,0:T(8,128)(2,1)} %param.7, bf16[1,48,64,64]{3,2,1,0:T(8,128)(2,1)S(1)} %collective-permute-done), kind=kLoop, calls=%fused_computation.23 | loop fusion | flops 1179648 | bytes 2359296 | tf_op jit(solution)/shard_map/concatenate | solution.py:22
  38.5 2.5 broadcast.135
  40.9 100.4 %while.13 = (s32[]{:T(128)}, f32[129,64,64]{2,1,0:T(8,128)}, s32[48,8]{1,0:T(8,128)S(1)}, bf16[48,8,64,64]{3,2,1,0:T(8,128)(2,1)}, s32[48,8]{1,0:T(8,128)S(1)}, ...) while((s32[]{:T(128)}, f32[129,64,64]{2,1,0:T(8,128)}, ...), condition=%wide.region_6.7_spmd, body=%wide.region_4.6_spmd.sunk | while | flops 135792768 | bytes 18100132 | solution.py:44
  41.0 0.1 reshape.233
  41.1 2.6 gather_fusion
  43.7 4.9 %fusion.34 = f32[16,8,64,64]{3,2,1,0:T(8,128)} fusion(bf16[16,8,64,64]{3,2,1,0:T(8,128)(2,1)S(1)} %bitcast.32, bf16[48,8,64,64]{3,2,1,0:T(8,128)(2,1)} %get-tuple-element.218, s32[]{:T(128)S(6)} %select_n.108, pred[16,8]{1,0:T(8,128)(4,1)S(1)} %get-tuple-element.192, bf16[48,64,64]{2,1,0:T(8,128)(2,1)} %get-tuple-element.221), kind=kOutput, calls=%fused_computation.5.clone.1 | convolution fusion | flops 135266304 | bytes 5506176 | tf_op jit(solution)/shard_map/while/body/eval_jaxpr/iba,ikbc->ikac/dot_general | solution.py:40
  48.6 5.6 %copy.31 = f32[128,64,64]{2,1,0:T(8,128)} copy(f32[128,64,64]{1,2,0:T(8,128)} %bitcast.31) | data formatting | bytes 4194304 | tf_op jit(solution)/shard_map/while/body/eval_jaxpr/reshape | solution.py:41
  54.2 0.1 reshape.232
  54.3 20.1 %scatter_fusion = f32[129,64,64]{2,1,0:T(8,128)} fusion(f32[129,64,64]{2,1,0:T(8,128)} %get-tuple-element.205, s32[128]{0:T(128)S(1)} %reshape.232, f32[128,64,64]{2,1,0:T(8,128)} %copy.31), kind=kCustom, calls=%fused_computation.1.clone.1 | custom fusion | flops 524288 | bytes 6291968 | tf_op jit(solution)/shard_map/while/body/eval_jaxpr/scatter-add | solution.py:41
  74.4 0.1 reshape.233
  74.5 2.6 gather_fusion
  77.1 4.9 %fusion.34 = f32[16,8,64,64]{3,2,1,0:T(8,128)} fusion(bf16[16,8,64,64]{3,2,1,0:T(8,128)(2,1)S(1)} %bitcast.32, bf16[48,8,64,64]{3,2,1,0:T(8,128)(2,1)} %get-tuple-element.218, s32[]{:T(128)S(6)} %select_n.108, pred[16,8]{1,0:T(8,128)(4,1)S(1)} %get-tuple-element.192, bf16[48,64,64]{2,1,0:T(8,128)(2,1)} %get-tuple-element.221), kind=kOutput, calls=%fused_computation.5.clone.1 | convolution fusion | flops 135266304 | bytes 5506176 | tf_op jit(solution)/shard_map/while/body/eval_jaxpr/iba,ikbc->ikac/dot_general | solution.py:40
  82.0 5.6 %copy.31 = f32[128,64,64]{2,1,0:T(8,128)} copy(f32[128,64,64]{1,2,0:T(8,128)} %bitcast.31) | data formatting | bytes 4194304 | tf_op jit(solution)/shard_map/while/body/eval_jaxpr/reshape | solution.py:41
  87.6 0.1 reshape.232
  87.7 20.1 %scatter_fusion = f32[129,64,64]{2,1,0:T(8,128)} fusion(f32[129,64,64]{2,1,0:T(8,128)} %get-tuple-element.205, s32[128]{0:T(128)S(1)} %reshape.232, f32[128,64,64]{2,1,0:T(8,128)} %copy.31), kind=kCustom, calls=%fused_computation.1.clone.1 | custom fusion | flops 524288 | bytes 6291968 | tf_op jit(solution)/shard_map/while/body/eval_jaxpr/scatter-add | solution.py:41
  107.8 0.1 reshape.233
  107.9 2.6 gather_fusion
  110.6 4.9 %fusion.34 = f32[16,8,64,64]{3,2,1,0:T(8,128)} fusion(bf16[16,8,64,64]{3,2,1,0:T(8,128)(2,1)S(1)} %bitcast.32, bf16[48,8,64,64]{3,2,1,0:T(8,128)(2,1)} %get-tuple-element.218, s32[]{:T(128)S(6)} %select_n.108, pred[16,8]{1,0:T(8,128)(4,1)S(1)} %get-tuple-element.192, bf16[48,64,64]{2,1,0:T(8,128)(2,1)} %get-tuple-element.221), kind=kOutput, calls=%fused_computation.5.clone.1 | convolution fusion | flops 135266304 | bytes 5506176 | tf_op jit(solution)/shard_map/while/body/eval_jaxpr/iba,ikbc->ikac/dot_general | solution.py:40
  115.4 5.6 %copy.31 = f32[128,64,64]{2,1,0:T(8,128)} copy(f32[128,64,64]{1,2,0:T(8,128)} %bitcast.31) | data formatting | bytes 4194304 | tf_op jit(solution)/shard_map/while/body/eval_jaxpr/reshape | solution.py:41
  121.1 0.1 reshape.232
  121.2 20.2 %scatter_fusion = f32[129,64,64]{2,1,0:T(8,128)} fusion(f32[129,64,64]{2,1,0:T(8,128)} %get-tuple-element.205, s32[128]{0:T(128)S(1)} %reshape.232, f32[128,64,64]{2,1,0:T(8,128)} %copy.31), kind=kCustom, calls=%fused_computation.1.clone.1 | custom fusion | flops 524288 | bytes 6291968 | tf_op jit(solution)/shard_map/while/body/eval_jaxpr/scatter-add | solution.py:41
  141.3 4.7 %slice.14 = f32[128,64,64]{2,1,0:T(8,128)} slice(f32[129,64,64]{2,1,0:T(8,128)} %get-tuple-element.129), slice={[0:128], [0:64], [0:64]} | slice | bytes 4194304 | tf_op jit(solution)/shard_map/slice | solution.py:70
  146.1 5.5 %reshape.220 = f32[16,1,32768]{2,1,0:T(1,128)} reshape(f32[16,8,64,64]{3,2,1,0:T(8,128)} %bitcast.36) | data formatting | bytes 4194304
  151.6 8.2 %all-to-all-start.1 = ((f32[16,1,32768]{2,1,0:T(1,128)}), f32[16,1,32768]{2,1,0:T(1,128)S(1)}, u32[]{:S(2)}, u32[]{:S(2)}) async-start(f32[16,1,32768]{2,1,0:T(1,128)} %reshape.220), calls=%async_computation.1 | async-start | bytes 4194304 | tf_op jit(solution)/shard_map/all_to_all | solution.py:73
  159.7 0.2 all-gather.2.cloned.1.call-start
  160.0 0.1 reshape.205
  160.1 48.7 %all-to-all-done.1 = f32[16,1,32768]{2,1,0:T(1,128)S(1)} async-done(((f32[16,1,32768]{2,1,0:T(1,128)}), f32[16,1,32768]{2,1,0:T(1,128)S(1)}, u32[]{:S(2)}, u32[]{:S(2)}) %all-to-all-start.1) | async-done | bytes 2097184 | tf_op jit(solution)/shard_map/all_to_all | solution.py:73
  208.8 1.3 copy-done
  210.1 0.6 broadcast.151
  210.7 7.3 %reduce = f32[16,32768]{1,0:T(8,128)S(1)} reduce(f32[16,1,32768]{2,1,0:T(1,128)} %copy-done, f32[]{:T(128)} %broadcast.151), dimensions={1}, to_apply=%all_to_all.8.reduce_sub_computation | reduce | bytes 4194308 | tf_op jit(solution)/shard_map/all_to_all | solution.py:73
  218.0 3.0 %reshape.221 = f32[16,8,64,64]{3,2,1,0:T(8,128)} reshape(f32[16,32768]{1,0:T(8,128)S(1)} %reduce) | data formatting | bytes 4194304
  221.1 13.5 %scatter_fusion.1 = f32[13,64,64]{2,1,0:T(8,128)S(1)} fusion(f32[13,64,64]{2,1,0:T(8,128)S(1)} %broadcast_in_dim.55, s32[128]{0:T(128)S(1)} %reshape.205, f32[128,64,64]{2,1,0:T(8,128)} %bitcast.35), kind=kCustom, calls=%fused_computation.4 | custom fusion | flops 524288 | bytes 6291968 | tf_op jit(solution)/shard_map/scatter-add | solution.py:78
  234.6 0.7 slice.20
  235.4 51.7 %all-gather.2.cloned.1.call-done = bf16[192,64,64]{2,1,0:T(8,128)(2,1)} async-done(((bf16[12,64,64]{2,1,0:T(8,128)(2,1)}), bf16[192,64,64]{2,1,0:T(8,128)(2,1)}) %all-gather.2.cloned.1.call-update) | async-done | bytes 1572880 | tf_op jit(solution)/shard_map/all_gather | solution.py:80
  287.0 5.2 %copy.27 = bf16[1,192,64,64]{1,3,2,0:T(8,128)(2,1)} copy(bf16[1,192,64,64]{3,2,1,0:T(8,128)(2,1)} %bitcast.38) | data formatting | bytes 3145728 | tf_op jit(solution)/shard_map/broadcast_in_dim | solution.py:81
  (28 shorter events, 0.4 us)
Async XLA Ops:
  6.5 28.8 %collective-permute-start = (bf16[1,48,64,64]{3,2,1,0:T(8,128)(2,1)}, bf16[1,48,64,64]{3,2,1,0:T(8,128)(2,1)S(1)}, u32[]{:S(2)}, u32[]{:S(2)}) collective-permute-start(bf16[1,48,64,64]{3,2,1,0:T(8,128)(2,1)} %param.7), channel_id=1, source_target_pairs={{0,16},{16,32},{32,48},{48,64},{64,80},{80,96},{96,112},{112,128},... | collective-permute-start | bytes 1179656 | tf_op jit(solution)/shard_map/ppermute | solution.py:20
  12.3 23.0 %collective-permute-start.1 = (bf16[1,48,64,64]{3,2,1,0:T(8,128)(2,1)}, bf16[1,48,64,64]{3,2,1,0:T(8,128)(2,1)S(1)}, u32[]{:S(2)}, u32[]{:S(2)}) collective-permute-start(bf16[1,48,64,64]{3,2,1,0:T(8,128)(2,1)} %param.7), channel_id=1, source_target_pairs={{16,0},{32,16},{48,32},{64,48},{80,64},{96,80},{112,96},{128,112},... | collective-permute-start | bytes 1179656 | tf_op jit(solution)/shard_map/ppermute | solution.py:21
  21.4 130.2 %all-to-all-start = ((s32[16,1,8]{2,1,0:T(1,128)}), s32[16,1,8]{2,1,0:T(1,128)S(1)}, u32[]{:S(2)}, u32[]{:S(2)}) async-start(s32[16,1,8]{2,1,0:T(1,128)} %bitcast.6), calls=%async_computation | async-start | bytes 16384 | tf_op jit(solution)/shard_map/all_to_all | solution.py:74
  151.6 57.2 %all-to-all-start.1 = ((f32[16,1,32768]{2,1,0:T(1,128)}), f32[16,1,32768]{2,1,0:T(1,128)S(1)}, u32[]{:S(2)}, u32[]{:S(2)}) async-start(f32[16,1,32768]{2,1,0:T(1,128)} %reshape.220), calls=%async_computation.1 | async-start | bytes 4194304 | tf_op jit(solution)/shard_map/all_to_all | solution.py:73
  159.7 127.3 %all-gather.2.cloned.1.call-start = ((), (), s32[]{:S(2)}) async-start(), calls=%async_computation.2 | async-start | bytes 3342336 | tf_op jit(solution)/shard_map/all_gather | solution.py:80
  208.8 1.3 copy-start
Sparse Core Ops, SparseCore 0:
  235.5 51.4 all-gather.1
where the time goes:
time: 301 us; the launch traced here: 299 us
  waiting for transfers between devices  100 us (33%)
  other arithmetic  91.1 us (30%)
  local copies, waits for them, and re-layouts  50.9 us (17%)
  starting transfers between devices  28.4 us (9%)
  matrix products  14.6 us (5%)
  between operations  13.5 us (4%)
    scatter-add x3, other arithmetic, one_step(): jax.ops.segment_sum(terms.reshape(-1, width, width), target_part, segments)  60.3 us
    all_gather x1, waiting for transfers between devices, body(): gathered = lax.all_gather(finished, 'sub', axis=0, tiled=True)  51.7 us
    all_to_all x1, waiting for transfers between devices, body(): lax.all_to_all(slots, 'sub', split_axis=0, concat_axis=0, tiled=True)  48.7 us
    reshape x3, local copies, waits for them, and re-layouts, one_step(): terms.reshape(-1, width, width)  16.9 us
    dot_general x3, matrix products, one_step(): jnp.einsum('iba,ikbc->ikac', row_part, product, preferred_element_type=jn...  14.6 us
    scatter-add x1, other arithmetic, body(): jax.ops.segment_sum(received.reshape(-1, width, width), local_ids, own + 1)  13.5 us
    all_to_all x1, starting transfers between devices, body(): lax.all_to_all(slot_tile, 'sub', split_axis=0, concat_axis=0, tiled=True)  12.9 us
    unnamed x6, local copies, waits for them, and re-layouts  11.3 us
  transfers between devices with their start and end apart: 5, of which 2 were waited for; matrix products, arithmetic and copies ran while one was open for 42% of the time, Pallas kernels for 0%

commit v1 on v0

v1 whole, which is shorter than its diff:
```python
import functools

import jax
import jax.numpy as jnp
from jax import lax
from jax.experimental import pallas as pl
from jax.experimental.pallas import tpu as pltpu
from jax.sharding import PartitionSpec as P

F32, BF16 = jnp.float32, jnp.bfloat16
ROWS = 8


def twice(x):
    return jnp.concatenate([x, x], axis=-1)


def galerkin(chip_core, cols, tiles, a_ref, p_ref, before_ref, after_ref, keep_ref, send_ref, near, acc):
    fine, width = p_ref.shape[0], p_ref.shape[1]
    half = fine // 2
    steps, own = pl.num_programs(0), pl.program_id(0)
    n_tiles = acc.shape[0] // width

    @pl.when(own == 0)
    def _():
        def clear(t, _):
            acc[pl.ds(pl.multiple_of(t * width, width), width), :] = jnp.zeros((width, 2 * width), F32)
            return 0

        lax.fori_loop(0, n_tiles, clear, 0, unroll=4)

        def fill(r, _):
            near[fine + r] = twice(p_ref[r])
            return 0

        lax.fori_loop(0, fine, fill, 0, unroll=4)

        def fill_ghost(r, _):
            for at, ref in ((0, before_ref), (2 * fine, after_ref)):
                both = ref[r]
                near[at + r] = twice(both[:, :width])
                near[at + half + r] = twice(both[:, width:])
            return 0

        lax.fori_loop(0, half, fill_ghost, 0, unroll=2)

    per_row = a_ref.shape[1]

    def one_row(r, _):
        i = own * ROWS + r
        left = p_ref[i].T
        terms = []
        for k in range(per_row):
            ap = jnp.dot(a_ref[r, k], near[cols[k, i]], preferred_element_type=F32).astype(BF16)
            terms.append(jnp.dot(left, ap, preferred_element_type=F32))
        for k in range(per_row):
            at = pl.ds(pl.multiple_of(tiles[k, i] * width, width), width)
            acc[at, :] += terms[k]
        return 0

    lax.fori_loop(0, ROWS, one_row, 0)

    @pl.when(own == steps - 1)
    def _():
        core = chip_core[0]
        low = lax.broadcasted_iota(jnp.int32, (n_tiles, 2 * width), 1) < width
        groups = keep_ref.shape[0]
        rows = width // (2 * groups)

        def pair(a):
            even = acc[pl.ds(a, n_tiles, stride=width), :]
            odd = acc[pl.ds(a + 1, n_tiles, stride=width), :]
            return jnp.where(low, even, odd)

        for y in range(groups):
            for p in range(rows // 2):
                base = 2 * rows * y + 2 * p
                at = slice(p * n_tiles, (p + 1) * n_tiles)
                keep_ref[y, at, :] = pair(base + rows * core)
                send_ref[y, at, :] = pair(base + rows * (1 - core)).astype(BF16)


def finish(got_ref, out_ref):
    peers, packed, lanes = got_ref.shape
    n_tiles = packed // 2
    total = got_ref[0].astype(F32)
    for y in range(1, peers):
        total = total + got_ref[y].astype(F32)
    first, second = total[:n_tiles], total[n_tiles:]
    rest = jnp.concatenate([first[lanes:], second[lanes:]], axis=0)
    block = jnp.concatenate([first[:lanes].T, second[:lanes].T, rest.T], axis=0).astype(BF16)
    for y in range(peers):
        out_ref[y] = block


def spread(chip_core, mine_ref, other_ref, out_ref):
    core = chip_core[0]
    packed, lanes = mine_ref.shape[1], mine_ref.shape[2]
    slab, half = out_ref.shape[0] // 2, lanes // 2
    for ref, at in ((mine_ref, core), (other_ref, 1 - core)):
        start = pl.multiple_of(at * slab, slab)
        out_ref[pl.ds(start, slab), 0:lanes] = ref[0, 0:slab, :]
        rest = ref[0, slab:packed, :]
        out_ref[pl.ds(start, lanes), lanes : lanes + half] = rest[:, :half]
        out_ref[pl.ds(start + lanes, lanes), lanes : lanes + half] = rest[:, half:]


def body(n_tiles, a_blocks, p_blocks, a_cols, tile_of_item):
    fine, per_row, width = a_blocks.shape[1], a_blocks.shape[2], a_blocks.shape[3]
    subs, doms = lax.axis_size("sub"), lax.axis_size("dom")
    chips = subs // 2
    lanes = 2 * width
    half = fine // 2
    core = (lax.axis_index("sub") % 2).astype(jnp.int32).reshape(1)
    own = p_blocks[0]
    cols, tiles = a_cols[0].T, tile_of_item[0].T

    up = [(d, d + 1) for d in range(doms - 1)]
    down = [(d + 1, d) for d in range(doms - 1)]
    swap = [(s, s ^ 1) for s in range(subs)]
    columns = [[2 * y + c for y in range(chips)] for c in range(2)]

    packed = jnp.concatenate([own[:half], own[half:]], axis=-1)
    before = lax.ppermute(packed, "dom", up)
    after = lax.ppermute(packed, "dom", down)

    whole = lambda shape: pl.BlockSpec(shape, lambda *_: (0,) * len(shape))
    share = width // subs // 2 * n_tiles
    keep, send = pl.pallas_call(
        galerkin,
        out_shape=(
            jax.ShapeDtypeStruct((chips, share, lanes), F32),
            jax.ShapeDtypeStruct((chips, share, lanes), BF16),
        ),
        grid_spec=pltpu.PrefetchScalarGridSpec(
            num_scalar_prefetch=3,
            grid=(fine // ROWS,),
            in_specs=[
                pl.BlockSpec((ROWS, per_row, width, width), lambda g, *_: (g, 0, 0, 0)),
                whole((fine, width, width)),
                whole((half, width, lanes)),
                whole((half, width, lanes)),
            ],
            out_specs=(whole((chips, share, lanes)), whole((chips, share, lanes))),
            scratch_shapes=[
                pltpu.VMEM((3 * fine, width, lanes), BF16),
                pltpu.VMEM((n_tiles * width, lanes), F32),
            ],
        ),
        name="galerkin",
    )(core, cols, tiles, a_blocks[0], own, before, after)

    other = lax.ppermute(send, "sub", swap)
    merged = (keep + other.astype(F32)).astype(BF16)
    got = lax.all_to_all(merged, "sub", 0, 0, axis_index_groups=columns, tiled=True)
    block = pl.pallas_call(
        finish, out_shape=jax.ShapeDtypeStruct((chips, share, lanes), BF16), name="finish"
    )(got)
    mine = lax.all_to_all(block, "sub", 0, 0, axis_index_groups=columns, tiled=True)
    theirs = lax.ppermute(mine, "sub", swap)
    slab = width * width // chips
    spec = pl.BlockSpec((1, share, lanes), lambda y, *_: (y, 0, 0))
    out = pl.pallas_call(
        spread,
        out_shape=jax.ShapeDtypeStruct((width * width, n_tiles), BF16),
        grid_spec=pltpu.PrefetchScalarGridSpec(
            num_scalar_prefetch=1,
            grid=(chips,),
            in_specs=[spec, spec],
            out_specs=pl.BlockSpec((slab, n_tiles), lambda y, *_: (y, 0)),
        ),
        name="spread",
    )(core, mine, theirs)
    return out.reshape(width, width, n_tiles).transpose(2, 0, 1)[None]


def solution(mesh):
    placed = (
        P("dom", "sub", None, None, None),
        P("dom", "sub", None, None),
        P("dom", "sub", None),
        P("dom", "sub", None),
    )
    n_tiles = 12 * mesh.shape["sub"]
    return jax.shard_map(
        functools.partial(body, n_tiles),
        mesh=mesh,
        in_specs=placed,
        out_specs=P("dom", None, None, None),
        check_vma=False,
    )
```

time: 301 us -> 137 us (0.46)
  the two profiles are of different devices: /device:TPU:1 before, /device:TPU:9 now
where the time goes in v1:
time: 137 us
  blocking collectives  53.7 us (39%)
  Pallas kernels  33.4 us (24%)
  starting transfers between devices  27.9 us (20%)
  waiting for transfers between devices  17 us (12%)
  local copies, waits for them, and re-layouts  2.84 us (2%)
  other arithmetic  1.83 us (1%)
    all_to_all x1, blocking collectives, body(): lax.all_to_all(merged, 'sub', 0, 0, axis_index_groups=columns, tiled=True)  29.5 us
    pallas_call x1, Pallas kernels, body(): pl.pallas_call(galerkin, out_shape=(jax.ShapeDtypeStruct((chips, share, l...  25.3 us
    all_to_all x1, blocking collectives, body(): lax.all_to_all(block, 'sub', 0, 0, axis_index_groups=columns, tiled=True)  24.2 us
    ppermute x1, starting transfers between devices, body(): after = lax.ppermute(packed, 'dom', down)  17 us
    ppermute x1, waiting for transfers between devices, body(): before = lax.ppermute(packed, 'dom', up)  7.15 us
    pallas_call x1, Pallas kernels, body(): pl.pallas_call(spread, out_shape=jax.ShapeDtypeStruct((width * width, n_t...  5.92 us
    ppermute x1, waiting for transfers between devices, body(): after = lax.ppermute(packed, 'dom', down)  5.84 us
    ppermute x1, starting transfers between devices, body(): theirs = lax.ppermute(mine, 'sub', swap)  5.23 us
  transfers between devices with their start and end apart: 4, of which 4 were waited for; matrix products, arithmetic and copies ran while one was open for 0% of the time, Pallas kernels for 0%

profile of v1, /device:TPU:9, one launch (start us, length us, event | category | flops | bytes accessed | tf_op | source)
XLA Modules:
  0.0 136.7 jit_solution(3856216144901251216)
XLA Ops:
  0.0 1.2 slice_bitcast_fusion.1
  1.2 0.2 pad_maximum_fusion
  1.4 17.0 %collective-permute-start.1 = (bf16[24,64,128]{2,1,0:T(8,128)(2,1)S(1)}, bf16[24,64,128]{2,1,0:T(8,128)(2,1)S(1)}, u32[]{:S(2)}, u32[]{:S(2)}) collective-permute-start(bf16[24,64,128]{2,1,0:T(8,128)(2,1)S(1)} %pad_maximum_fusion), channel_id=1, source_target_pairs={{16,0},{32,16},{48,32},{64,48},{80,64},{96,80},{112,96},{128,112},... | collective-permute-start | bytes 1179656 | tf_op jit(solution)/shard_map/ppermute | solution.py:125
  18.4 1.9 %collective-permute-start = (bf16[24,64,128]{2,1,0:T(8,128)(2,1)S(1)}, bf16[24,64,128]{2,1,0:T(8,128)(2,1)S(1)}, u32[]{:S(2)}, u32[]{:S(2)}) collective-permute-start(bf16[24,64,128]{2,1,0:T(8,128)(2,1)S(1)} %pad_maximum_fusion), channel_id=1, source_target_pairs={{0,16},{16,32},{32,48},{48,64},{64,80},{80,96},{96,112},{112,128},... | collective-permute-start | bytes 1179656 | tf_op jit(solution)/shard_map/ppermute | solution.py:124
  20.4 5.8 %collective-permute-done.1.after_ref = bf16[24,64,128]{2,1,0:T(8,128)(2,1)S(1)} collective-permute-done((bf16[24,64,128]{2,1,0:T(8,128)(2,1)S(1)}, bf16[24,64,128]{2,1,0:T(8,128)(2,1)S(1)}, u32[]{:S(2)}, u32[]{:S(2)}) %collective-permute-start.1) | collective-permute-done | bytes 393248 | tf_op jit(solution)/shard_map/ppermute | solution.py:125
  26.2 0.0 copy-start.2
  26.2 7.2 %collective-permute-done.before_ref = bf16[24,64,128]{2,1,0:T(8,128)(2,1)S(1)} collective-permute-done((bf16[24,64,128]{2,1,0:T(8,128)(2,1)S(1)}, bf16[24,64,128]{2,1,0:T(8,128)(2,1)S(1)}, u32[]{:S(2)}, u32[]{:S(2)}) %collective-permute-start) | collective-permute-done | bytes 393248 | tf_op jit(solution)/shard_map/ppermute | solution.py:124
  33.3 0.0 copy-start.3
  33.3 0.0 copy-done.2
  33.4 0.8 copy-done.3
  34.1 25.3 %galerkin.1 = (f32[8,384,128]{2,1,0:T(8,128)}, bf16[8,384,128]{2,1,0:T(8,128)(2,1)}) custom-call(s32[1]{0:T(128)} %bitcast.chip_core, s32[8,48]{1,0:T(8,128)} %bitcast.20, s32[8,48]{1,0:T(8,128)} %bitcast.21, bf16[48,8,64,64]{3,2,1,0:T(8,128)(2,1)} %bitcast.18, bf16[48,64,64]{2,1,0:T(8,128)(2,1)} %bitcast.19, bf16[24,64,128]{2,1,0:T(8,128)(2,1)} %copy-done.3, ...), custom_call_target="tpu_custom_call" | custom-call | tf_op jit(solution)/shard_map/galerkin/pallas_call | solution.py:129
  59.4 3.7 %collective-permute-start.2 = (bf16[8,384,128]{2,1,0:T(8,128)(2,1)}, bf16[8,384,128]{2,1,0:T(8,128)(2,1)S(1)}, u32[]{:S(2)}, u32[]{:S(2)}) collective-permute-start(bf16[8,384,128]{2,1,0:T(8,128)(2,1)} %get-tuple-element.8), channel_id=1, source_target_pairs={{0,1},{1,0},{2,3},{3,2},{4,5},{5,4},{6,7},{7,6},{8,9},{9,8},{10,11... | collective-permute-start | bytes 2359304 | tf_op jit(solution)/shard_map/ppermute | solution.py:153
  63.1 2.1 %collective-permute-done.2 = bf16[8,384,128]{2,1,0:T(8,128)(2,1)S(1)} collective-permute-done((bf16[8,384,128]{2,1,0:T(8,128)(2,1)}, bf16[8,384,128]{2,1,0:T(8,128)(2,1)S(1)}, u32[]{:S(2)}, u32[]{:S(2)}) %collective-permute-start.2) | collective-permute-done | bytes 786464 | tf_op jit(solution)/shard_map/ppermute | solution.py:153
  65.2 1.6 %add_convert_fusion = bf16[8,384,128]{2,1,0:T(8,128)(2,1)S(1)} fusion(f32[8,384,128]{2,1,0:T(8,128)} %get-tuple-element.7, bf16[8,384,128]{2,1,0:T(8,128)(2,1)S(1)} %collective-permute-done.2), kind=kLoop, calls=%fused_computation | loop fusion | flops 1179648 | bytes 3145728 | tf_op jit(solution)/shard_map/convert_element_type | solution.py:154
  66.8 29.5 %all_to_all.10.got_ref = bf16[8,384,128]{2,1,0:T(8,128)(2,1)} all-to-all(bf16[8,384,128]{2,1,0:T(8,128)(2,1)S(1)} %add_convert_fusion), channel_id=1, replica_groups={{0,2,4,6,8,10,12,14},{1,3,5,7,9,11,13,15},{16,18,20,22,24,26,28,30},{17..., dimensions={0} | all-to-all | bytes 1572864 | tf_op jit(solution)/shard_map/all_to_all | solution.py:155
  96.3 2.2 %finish.1 = bf16[8,384,128]{2,1,0:T(8,128)(2,1)} custom-call(bf16[8,384,128]{2,1,0:T(8,128)(2,1)} %all_to_all.10.got_ref), custom_call_target="tpu_custom_call" | custom-call | tf_op jit(solution)/shard_map/finish/pallas_call | solution.py:156
  98.6 24.2 %all_to_all.11.mine_ref = bf16[8,384,128]{2,1,0:T(8,128)(2,1)S(1)} all-to-all(bf16[8,384,128]{2,1,0:T(8,128)(2,1)} %finish.1), channel_id=1, replica_groups={{0,2,4,6,8,10,12,14},{1,3,5,7,9,11,13,15},{16,18,20,22,24,26,28,30},{17..., dimensions={0} | all-to-all | bytes 1572864 | tf_op jit(solution)/shard_map/all_to_all | solution.py:159
  122.8 0.0 copy-start
  122.8 5.2 %collective-permute-start.3 = (bf16[8,384,128]{2,1,0:T(8,128)(2,1)S(1)}, bf16[8,384,128]{2,1,0:T(8,128)(2,1)S(1)}, u32[]{:S(2)}, u32[]{:S(2)}) collective-permute-start(bf16[8,384,128]{2,1,0:T(8,128)(2,1)S(1)} %all_to_all.11.mine_ref), channel_id=1, source_target_pairs={{0,1},{1,0},{2,3},{3,2},{4,5},{5,4},{6,7},{7,6},{8,9},{9,8},{10,11... | collective-permute-start | bytes 2359304 | tf_op jit(solution)/shard_map/ppermute | solution.py:160
  128.0 1.9 %collective-permute-done.3.other_ref = bf16[8,384,128]{2,1,0:T(8,128)(2,1)S(1)} collective-permute-done((bf16[8,384,128]{2,1,0:T(8,128)(2,1)S(1)}, bf16[8,384,128]{2,1,0:T(8,128)(2,1)S(1)}, u32[]{:S(2)}, u32[]{:S(2)}) %collective-permute-start.3) | collective-permute-done | bytes 786464 | tf_op jit(solution)/shard_map/ppermute | solution.py:160
  129.9 0.0 copy-done
  129.9 0.0 copy-start.1
  129.9 0.9 copy-done.1
  130.8 5.9 %spread.1 = bf16[4096,192]{1,0:T(8,128)(2,1)} custom-call(s32[1]{0:T(128)} %bitcast.chip_core, bf16[8,384,128]{2,1,0:T(8,128)(2,1)} %copy-done, bf16[8,384,128]{2,1,0:T(8,128)(2,1)} %copy-done.1), custom_call_target="tpu_custom_call" | custom-call | tf_op jit(solution)/shard_map/spread/pallas_call | solution.py:163
Async XLA Ops:
  1.4 24.8 %collective-permute-start.1 = (bf16[24,64,128]{2,1,0:T(8,128)(2,1)S(1)}, bf16[24,64,128]{2,1,0:T(8,128)(2,1)S(1)}, u32[]{:S(2)}, u32[]{:S(2)}) collective-permute-start(bf16[24,64,128]{2,1,0:T(8,128)(2,1)S(1)} %pad_maximum_fusion), channel_id=1, source_target_pairs={{16,0},{32,16},{48,32},{64,48},{80,64},{96,80},{112,96},{128,112},... | collective-permute-start | bytes 1179656 | tf_op jit(solution)/shard_map/ppermute | solution.py:125
  18.4 14.9 %collective-permute-start = (bf16[24,64,128]{2,1,0:T(8,128)(2,1)S(1)}, bf16[24,64,128]{2,1,0:T(8,128)(2,1)S(1)}, u32[]{:S(2)}, u32[]{:S(2)}) collective-permute-start(bf16[24,64,128]{2,1,0:T(8,128)(2,1)S(1)} %pad_maximum_fusion), channel_id=1, source_target_pairs={{0,16},{16,32},{32,48},{48,64},{64,80},{80,96},{96,112},{112,128},... | collective-permute-start | bytes 1179656 | tf_op jit(solution)/shard_map/ppermute | solution.py:124
  26.2 7.2 %copy-start.2 = (bf16[24,64,128]{2,1,0:T(8,128)(2,1)}, bf16[24,64,128]{2,1,0:T(8,128)(2,1)S(1)}, u32[]{:S(2)}) copy-start(bf16[24,64,128]{2,1,0:T(8,128)(2,1)S(1)} %collective-permute-done.1.after_ref) | copy-start | bytes 1179652
  33.3 0.8 copy-start.3
  59.4 5.8 %collective-permute-start.2 = (bf16[8,384,128]{2,1,0:T(8,128)(2,1)}, bf16[8,384,128]{2,1,0:T(8,128)(2,1)S(1)}, u32[]{:S(2)}, u32[]{:S(2)}) collective-permute-start(bf16[8,384,128]{2,1,0:T(8,128)(2,1)} %get-tuple-element.8), channel_id=1, source_target_pairs={{0,1},{1,0},{2,3},{3,2},{4,5},{5,4},{6,7},{7,6},{8,9},{9,8},{10,11... | collective-permute-start | bytes 2359304 | tf_op jit(solution)/shard_map/ppermute | solution.py:153
  122.8 7.1 %copy-start = (bf16[8,384,128]{2,1,0:T(8,128)(2,1)}, bf16[8,384,128]{2,1,0:T(8,128)(2,1)S(1)}, u32[]{:S(2)}) copy-start(bf16[8,384,128]{2,1,0:T(8,128)(2,1)S(1)} %all_to_all.11.mine_ref) | copy-start | bytes 2359300
  122.8 7.1 %collective-permute-start.3 = (bf16[8,384,128]{2,1,0:T(8,128)(2,1)S(1)}, bf16[8,384,128]{2,1,0:T(8,128)(2,1)S(1)}, u32[]{:S(2)}, u32[]{:S(2)}) collective-permute-start(bf16[8,384,128]{2,1,0:T(8,128)(2,1)S(1)} %all_to_all.11.mine_ref), channel_id=1, source_target_pairs={{0,1},{1,0},{2,3},{3,2},{4,5},{5,4},{6,7},{7,6},{8,9},{9,8},{10,11... | collective-permute-start | bytes 2359304 | tf_op jit(solution)/shard_map/ppermute | solution.py:160
  129.9 0.9 copy-start.1

commit v2 on v1

--- a/solution.py
+++ b/solution.py
@@ -9,6 +9,7 @@
 
 F32, BF16 = jnp.float32, jnp.bfloat16
 ROWS = 8
+UNROLL = 8
 
 
 def twice(x):
@@ -50,59 +51,93 @@
         i = own * ROWS + r
         left = p_ref[i].T
         terms = []
-        for k in range(per_row):
-            ap = jnp.dot(a_ref[r, k], near[cols[k, i]], preferred_element_type=F32).astype(BF16)
-            terms.append(jnp.dot(left, ap, preferred_element_type=F32))
+        for k in range(0, per_row, 2):
+            ap = [
+                jnp.dot(a_ref[r, q], near[cols[q, i]], preferred_element_type=F32).astype(BF16)
+                for q in (k, k + 1)
+            ]
+            both = jnp.dot(left, jnp.concatenate(ap, axis=1), preferred_element_type=F32)
+            terms += [both[:, : 2 * width], both[:, 2 * width :]]
         for k in range(per_row):
             at = pl.ds(pl.multiple_of(tiles[k, i] * width, width), width)
             acc[at, :] += terms[k]
         return 0
 
-    lax.fori_loop(0, ROWS, one_row, 0)
+    lax.fori_loop(0, ROWS, one_row, 0, unroll=UNROLL)
 
     @pl.when(own == steps - 1)
     def _():
-        core = chip_core[0]
-        low = lax.broadcasted_iota(jnp.int32, (n_tiles, 2 * width), 1) < width
-        groups = keep_ref.shape[0]
-        rows = width // (2 * groups)
-
-        def pair(a):
-            even = acc[pl.ds(a, n_tiles, stride=width), :]
-            odd = acc[pl.ds(a + 1, n_tiles, stride=width), :]
-            return jnp.where(low, even, odd)
-
-        for y in range(groups):
-            for p in range(rows // 2):
-                base = 2 * rows * y + 2 * p
-                at = slice(p * n_tiles, (p + 1) * n_tiles)
-                keep_ref[y, at, :] = pair(base + rows * core)
-                send_ref[y, at, :] = pair(base + rows * (1 - core)).astype(BF16)
-
-
-def finish(got_ref, out_ref):
+        first_core = lax.broadcasted_iota(jnp.int32, (8, 2 * width), 0) * 0 + chip_core[0] == 0
+        left_half = lax.broadcasted_iota(jnp.int32, (8, 2 * width), 1) < width
+        upper = lax.broadcasted_iota(jnp.int32, (8, 2 * width), 0) < 4
+        groups, quads = keep_ref.shape[0], n_tiles // 4
+
+        def pack(u, _):
+            for y in range(groups):
+                rows = []
+                for w in range(2):
+                    def tile(q):
+                        start = (2 * u + w + q * quads) * width + 8 * y
+                        return acc[pl.ds(pl.multiple_of(start, 8), 8), :]
+
+                    even = jnp.where(left_half, tile(0), tile(2))
+                    odd = jnp.where(left_half, tile(1), tile(3))
+                    top = jnp.where(upper, even, pltpu.roll(odd, 4, 0))
+                    bottom = jnp.where(upper, pltpu.roll(even, 4, 0), odd)
+                    rows.append((jnp.where(first_core, top, bottom), jnp.where(first_core, bottom, top)))
+                at = pl.ds(pl.multiple_of(16 * u, 16), 16)
+                keep_ref[y, at, :] = jnp.concatenate([rows[0][0], rows[1][0]], axis=0)
+                send_ref[y, at, :] = jnp.concatenate([rows[0][1], rows[1][1]], axis=0).astype(BF16)
+            return 0
+
+        lax.fori_loop(0, quads // 2, pack, 0, unroll=2)
+
+
+def finish(got_ref, out_ref, total):
     peers, packed, lanes = got_ref.shape
-    n_tiles = packed // 2
-    total = got_ref[0].astype(F32)
+    half, quads = lanes // 2, packed // 8
+    n_tiles = 4 * quads
+    sums = got_ref[0].astype(F32)
     for y in range(1, peers):
-        total = total + got_ref[y].astype(F32)
-    first, second = total[:n_tiles], total[n_tiles:]
-    rest = jnp.concatenate([first[lanes:], second[lanes:]], axis=0)
-    block = jnp.concatenate([first[:lanes].T, second[:lanes].T, rest.T], axis=0).astype(BF16)
+        sums = sums + got_ref[y].astype(F32)
+    total[...] = sums
+    slab = []
+    for r in range(4):
+        rows = [total[pl.ds(4 * s + r, quads, stride=8), :] for s in range(2)]
+        turned = jnp.concatenate(rows, axis=0).T
+        slab.append(jnp.concatenate([turned[:half], turned[half:]], axis=1))
+    slab = jnp.concatenate(slab, axis=0)
+    rest = jnp.concatenate([slab[:lanes, lanes:], slab[lanes:, lanes:]], axis=1)
+    block = jnp.concatenate([slab[:, :lanes], rest], axis=0).astype(BF16)
     for y in range(peers):
         out_ref[y] = block
 
 
-def spread(chip_core, mine_ref, other_ref, out_ref):
-    core = chip_core[0]
-    packed, lanes = mine_ref.shape[1], mine_ref.shape[2]
-    slab, half = out_ref.shape[0] // 2, lanes // 2
-    for ref, at in ((mine_ref, core), (other_ref, 1 - core)):
-        start = pl.multiple_of(at * slab, slab)
-        out_ref[pl.ds(start, slab), 0:lanes] = ref[0, 0:slab, :]
-        rest = ref[0, slab:packed, :]
-        out_ref[pl.ds(start, lanes), lanes : lanes + half] = rest[:, :half]
-        out_ref[pl.ds(start + lanes, lanes), lanes : lanes + half] = rest[:, half:]
+def spread(mine_hbm, other_hbm, out_hbm, mine, other, out, got_sem, put_sem):
+    core = lax.axis_index("sub") % 2
+    chips, packed, lanes = mine.shape
+    slab, half = out.shape[0] // (2 * chips), lanes // 2
+    fetch = lambda y: [
+        pltpu.make_async_copy(src.at[y], dst.at[y], got_sem.at[i, y])
+        for i, (src, dst) in enumerate(((mine_hbm, mine), (other_hbm, other)))
+    ]
+    put = lambda y: pltpu.make_async_copy(
+        out.at[pl.ds(2 * slab * y, 2 * slab)], out_hbm.at[pl.ds(2 * slab * y, 2 * slab)], put_sem.at[y]
+    )
+    for y in range(chips):
+        for copy in fetch(y):
+            copy.start()
+    for y in range(chips):
+        for copy, ref, at in zip(fetch(y), (mine, other), (core, 1 - core)):
+            copy.wait()
+            start = pl.multiple_of((2 * y + at) * slab, slab)
+            out[pl.ds(start, slab), 0:lanes] = ref[y, 0:slab, :]
+            rest = ref[y, slab:packed, :]
+            out[pl.ds(start, lanes), lanes : lanes + half] = rest[:, :half]
+            out[pl.ds(start + lanes, lanes), lanes : lanes + half] = rest[:, half:]
+        put(y).start()
+    for y in range(chips):
+        put(y).wait()
 
 
 def body(n_tiles, a_blocks, p_blocks, a_cols, tile_of_item):
@@ -154,23 +189,30 @@
     merged = (keep + other.astype(F32)).astype(BF16)
     got = lax.all_to_all(merged, "sub", 0, 0, axis_index_groups=columns, tiled=True)
     block = pl.pallas_call(
-        finish, out_shape=jax.ShapeDtypeStruct((chips, share, lanes), BF16), name="finish"
+        finish,
+        out_shape=jax.ShapeDtypeStruct((chips, share, lanes), BF16),
+        scratch_shapes=[pltpu.VMEM((share, lanes), F32)],
+        compiler_params=pltpu.CompilerParams(vmem_limit_bytes=8 << 20),
+        name="finish",
     )(got)
     mine = lax.all_to_all(block, "sub", 0, 0, axis_index_groups=columns, tiled=True)
     theirs = lax.ppermute(mine, "sub", swap)
-    slab = width * width // chips
-    spec = pl.BlockSpec((1, share, lanes), lambda y, *_: (y, 0, 0))
+    anywhere = pl.BlockSpec(memory_space=pl.ANY)
     out = pl.pallas_call(
         spread,
         out_shape=jax.ShapeDtypeStruct((width * width, n_tiles), BF16),
-        grid_spec=pltpu.PrefetchScalarGridSpec(
-            num_scalar_prefetch=1,
-            grid=(chips,),
-            in_specs=[spec, spec],
-            out_specs=pl.BlockSpec((slab, n_tiles), lambda y, *_: (y, 0)),
-        ),
+        in_specs=[anywhere, anywhere],
+        out_specs=anywhere,
+        scratch_shapes=[
+            pltpu.VMEM((chips, share, lanes), BF16),
+            pltpu.VMEM((chips, share, lanes), BF16),
+            pltpu.VMEM((width * width, n_tiles), BF16),
+            pltpu.SemaphoreType.DMA((2, chips)),
+            pltpu.SemaphoreType.DMA((chips,)),
+        ],
+        compiler_params=pltpu.CompilerParams(vmem_limit_bytes=12 << 20),
         name="spread",
-    )(core, mine, theirs)
+    )(mine, theirs)
     return out.reshape(width, width, n_tiles).transpose(2, 0, 1)[None]
 
 

time: 137 us -> 119 us (0.87)
  Pallas kernels: 33.4 us -> 17.6 us
    pallas_call x1, Pallas kernels: 25.3 us -> 12.9 us  [body(): pl.pallas_call(galerkin, out_shape=(jax.ShapeDtypeStruct((chips, share, l...]
    pallas_call x1, Pallas kernels: 2.24 us -> 0.35 us  [body(): pl.pallas_call(finish, out_shape=jax.ShapeDtypeStruct((chips, share, lane...]
    pallas_call x1, Pallas kernels: 5.92 us -> 4.36 us  [body(): pl.pallas_call(spread, out_shape=jax.ShapeDtypeStruct((width * width, n_t...]
where the time goes in v2:
time: 119 us
  blocking collectives  52.6 us (44%)
  starting transfers between devices  27.9 us (23%)
  Pallas kernels  17.6 us (15%)
  waiting for transfers between devices  17 us (14%)
  local copies, waits for them, and re-layouts  1.93 us (2%)
  other arithmetic  1.83 us (2%)
    all_to_all x1, blocking collectives, body(): lax.all_to_all(merged, 'sub', 0, 0, axis_index_groups=columns, tiled=True)  29.4 us
    all_to_all x1, blocking collectives, body(): lax.all_to_all(block, 'sub', 0, 0, axis_index_groups=columns, tiled=True)  23.1 us
    ppermute x1, starting transfers between devices, body(): after = lax.ppermute(packed, 'dom', down)  17 us
    pallas_call x1, Pallas kernels, body(): pl.pallas_call(galerkin, out_shape=(jax.ShapeDtypeStruct((chips, share, l...  12.9 us
    ppermute x1, waiting for transfers between devices, body(): before = lax.ppermute(packed, 'dom', up)  7.15 us
    ppermute x1, waiting for transfers between devices, body(): after = lax.ppermute(packed, 'dom', down)  5.84 us
    ppermute x1, starting transfers between devices, body(): theirs = lax.ppermute(mine, 'sub', swap)  5.23 us
    pallas_call x1, Pallas kernels, body(): pl.pallas_call(spread, out_shape=jax.ShapeDtypeStruct((width * width, n_t...  4.36 us
  transfers between devices with their start and end apart: 4, of which 4 were waited for; matrix products, arithmetic and copies ran while one was open for 0% of the time, Pallas kernels for 0%

profile of v2, /device:TPU:9, one launch (start us, length us, event | category | flops | bytes accessed | tf_op | source)
XLA Modules:
  0.0 118.8 jit_solution(13816696102339123322)
XLA Ops:
  0.0 1.2 slice_bitcast_fusion.1
  1.2 0.2 pad_maximum_fusion
  1.4 17.0 %collective-permute-start.1 = (bf16[24,64,128]{2,1,0:T(8,128)(2,1)S(1)}, bf16[24,64,128]{2,1,0:T(8,128)(2,1)S(1)}, u32[]{:S(2)}, u32[]{:S(2)}) collective-permute-start(bf16[24,64,128]{2,1,0:T(8,128)(2,1)S(1)} %pad_maximum_fusion), channel_id=1, source_target_pairs={{16,0},{32,16},{48,32},{64,48},{80,64},{96,80},{112,96},{128,112},... | collective-permute-start | bytes 1179656 | tf_op jit(solution)/shard_map/ppermute | solution.py:160
  18.4 1.9 %collective-permute-start = (bf16[24,64,128]{2,1,0:T(8,128)(2,1)S(1)}, bf16[24,64,128]{2,1,0:T(8,128)(2,1)S(1)}, u32[]{:S(2)}, u32[]{:S(2)}) collective-permute-start(bf16[24,64,128]{2,1,0:T(8,128)(2,1)S(1)} %pad_maximum_fusion), channel_id=1, source_target_pairs={{0,16},{16,32},{32,48},{48,64},{64,80},{80,96},{96,112},{112,128},... | collective-permute-start | bytes 1179656 | tf_op jit(solution)/shard_map/ppermute | solution.py:159
  20.4 5.8 %collective-permute-done.1.after_ref = bf16[24,64,128]{2,1,0:T(8,128)(2,1)S(1)} collective-permute-done((bf16[24,64,128]{2,1,0:T(8,128)(2,1)S(1)}, bf16[24,64,128]{2,1,0:T(8,128)(2,1)S(1)}, u32[]{:S(2)}, u32[]{:S(2)}) %collective-permute-start.1) | collective-permute-done | bytes 393248 | tf_op jit(solution)/shard_map/ppermute | solution.py:160
  26.2 0.0 copy-start
  26.2 7.2 %collective-permute-done.before_ref = bf16[24,64,128]{2,1,0:T(8,128)(2,1)S(1)} collective-permute-done((bf16[24,64,128]{2,1,0:T(8,128)(2,1)S(1)}, bf16[24,64,128]{2,1,0:T(8,128)(2,1)S(1)}, u32[]{:S(2)}, u32[]{:S(2)}) %collective-permute-start) | collective-permute-done | bytes 393248 | tf_op jit(solution)/shard_map/ppermute | solution.py:159
  33.3 0.0 copy-start.1
  33.3 0.0 copy-done
  33.4 0.8 copy-done.1
  34.1 12.9 %galerkin.1 = (f32[8,384,128]{2,1,0:T(8,128)}, bf16[8,384,128]{2,1,0:T(8,128)(2,1)}) custom-call(s32[1]{0:T(128)} %bitcast.chip_core, s32[8,48]{1,0:T(8,128)} %bitcast.20, s32[8,48]{1,0:T(8,128)} %bitcast.21, bf16[48,8,64,64]{3,2,1,0:T(8,128)(2,1)} %bitcast.18, bf16[48,64,64]{2,1,0:T(8,128)(2,1)} %bitcast.19, bf16[24,64,128]{2,1,0:T(8,128)(2,1)} %copy-done.1, ...), custom_call_target="tpu_custom_call" | custom-call | tf_op jit(solution)/shard_map/galerkin/pallas_call | solution.py:164
  47.0 3.7 %collective-permute-start.2 = (bf16[8,384,128]{2,1,0:T(8,128)(2,1)}, bf16[8,384,128]{2,1,0:T(8,128)(2,1)S(1)}, u32[]{:S(2)}, u32[]{:S(2)}) collective-permute-start(bf16[8,384,128]{2,1,0:T(8,128)(2,1)} %get-tuple-element.8), channel_id=1, source_target_pairs={{0,1},{1,0},{2,3},{3,2},{4,5},{5,4},{6,7},{7,6},{8,9},{9,8},{10,11... | collective-permute-start | bytes 2359304 | tf_op jit(solution)/shard_map/ppermute | solution.py:188
  50.7 2.1 %collective-permute-done.2 = bf16[8,384,128]{2,1,0:T(8,128)(2,1)S(1)} collective-permute-done((bf16[8,384,128]{2,1,0:T(8,128)(2,1)}, bf16[8,384,128]{2,1,0:T(8,128)(2,1)S(1)}, u32[]{:S(2)}, u32[]{:S(2)}) %collective-permute-start.2) | collective-permute-done | bytes 786464 | tf_op jit(solution)/shard_map/ppermute | solution.py:188
  52.8 1.6 %add_convert_fusion = bf16[8,384,128]{2,1,0:T(8,128)(2,1)S(1)} fusion(f32[8,384,128]{2,1,0:T(8,128)} %get-tuple-element.7, bf16[8,384,128]{2,1,0:T(8,128)(2,1)S(1)} %collective-permute-done.2), kind=kLoop, calls=%fused_computation | loop fusion | flops 1179648 | bytes 3145728 | tf_op jit(solution)/shard_map/convert_element_type | solution.py:189
  54.4 29.4 %all_to_all.10.got_ref = bf16[8,384,128]{2,1,0:T(8,128)(2,1)S(1)} all-to-all(bf16[8,384,128]{2,1,0:T(8,128)(2,1)S(1)} %add_convert_fusion), channel_id=1, replica_groups={{0,2,4,6,8,10,12,14},{1,3,5,7,9,11,13,15},{16,18,20,22,24,26,28,30},{17..., dimensions={0} | all-to-all | bytes 1572864 | tf_op jit(solution)/shard_map/all_to_all | solution.py:190
  83.8 0.4 finish.1
  84.2 23.1 %all_to_all.11.mine_hbm = bf16[8,384,128]{2,1,0:T(8,128)(2,1)S(1)} all-to-all(bf16[8,384,128]{2,1,0:T(8,128)(2,1)S(1)} %finish.1), channel_id=1, replica_groups={{0,2,4,6,8,10,12,14},{1,3,5,7,9,11,13,15},{16,18,20,22,24,26,28,30},{17..., dimensions={0} | all-to-all | bytes 1572864 | tf_op jit(solution)/shard_map/all_to_all | solution.py:198
  107.3 5.2 %collective-permute-start.3 = (bf16[8,384,128]{2,1,0:T(8,128)(2,1)S(1)}, bf16[8,384,128]{2,1,0:T(8,128)(2,1)S(1)}, u32[]{:S(2)}, u32[]{:S(2)}) collective-permute-start(bf16[8,384,128]{2,1,0:T(8,128)(2,1)S(1)} %all_to_all.11.mine_hbm), channel_id=1, source_target_pairs={{0,1},{1,0},{2,3},{3,2},{4,5},{5,4},{6,7},{7,6},{8,9},{9,8},{10,11... | collective-permute-start | bytes 2359304 | tf_op jit(solution)/shard_map/ppermute | solution.py:199
  112.6 1.9 %collective-permute-done.3.other_hbm = bf16[8,384,128]{2,1,0:T(8,128)(2,1)S(1)} collective-permute-done((bf16[8,384,128]{2,1,0:T(8,128)(2,1)S(1)}, bf16[8,384,128]{2,1,0:T(8,128)(2,1)S(1)}, u32[]{:S(2)}, u32[]{:S(2)}) %collective-permute-start.3) | collective-permute-done | bytes 786464 | tf_op jit(solution)/shard_map/ppermute | solution.py:199
  114.5 4.4 %spread.1 = bf16[4096,192]{1,0:T(8,128)(2,1)} custom-call(bf16[8,384,128]{2,1,0:T(8,128)(2,1)S(1)} %all_to_all.11.mine_hbm, bf16[8,384,128]{2,1,0:T(8,128)(2,1)S(1)} %collective-permute-done.3.other_hbm), custom_call_target="tpu_custom_call" | custom-call | tf_op jit(solution)/shard_map/spread/pallas_call | solution.py:201
Async XLA Ops:
  1.4 24.8 %collective-permute-start.1 = (bf16[24,64,128]{2,1,0:T(8,128)(2,1)S(1)}, bf16[24,64,128]{2,1,0:T(8,128)(2,1)S(1)}, u32[]{:S(2)}, u32[]{:S(2)}) collective-permute-start(bf16[24,64,128]{2,1,0:T(8,128)(2,1)S(1)} %pad_maximum_fusion), channel_id=1, source_target_pairs={{16,0},{32,16},{48,32},{64,48},{80,64},{96,80},{112,96},{128,112},... | collective-permute-start | bytes 1179656 | tf_op jit(solution)/shard_map/ppermute | solution.py:160
  18.4 14.9 %collective-permute-start = (bf16[24,64,128]{2,1,0:T(8,128)(2,1)S(1)}, bf16[24,64,128]{2,1,0:T(8,128)(2,1)S(1)}, u32[]{:S(2)}, u32[]{:S(2)}) collective-permute-start(bf16[24,64,128]{2,1,0:T(8,128)(2,1)S(1)} %pad_maximum_fusion), channel_id=1, source_target_pairs={{0,16},{16,32},{32,48},{48,64},{64,80},{80,96},{96,112},{112,128},... | collective-permute-start | bytes 1179656 | tf_op jit(solution)/shard_map/ppermute | solution.py:159
  26.2 7.2 %copy-start = (bf16[24,64,128]{2,1,0:T(8,128)(2,1)}, bf16[24,64,128]{2,1,0:T(8,128)(2,1)S(1)}, u32[]{:S(2)}) copy-start(bf16[24,64,128]{2,1,0:T(8,128)(2,1)S(1)} %collective-permute-done.1.after_ref) | copy-start | bytes 1179652
  33.3 0.8 copy-start.1
  47.0 5.8 %collective-permute-start.2 = (bf16[8,384,128]{2,1,0:T(8,128)(2,1)}, bf16[8,384,128]{2,1,0:T(8,128)(2,1)S(1)}, u32[]{:S(2)}, u32[]{:S(2)}) collective-permute-start(bf16[8,384,128]{2,1,0:T(8,128)(2,1)} %get-tuple-element.8), channel_id=1, source_target_pairs={{0,1},{1,0},{2,3},{3,2},{4,5},{5,4},{6,7},{7,6},{8,9},{9,8},{10,11... | collective-permute-start | bytes 2359304 | tf_op jit(solution)/shard_map/ppermute | solution.py:188
  107.3 7.1 %collective-permute-start.3 = (bf16[8,384,128]{2,1,0:T(8,128)(2,1)S(1)}, bf16[8,384,128]{2,1,0:T(8,128)(2,1)S(1)}, u32[]{:S(2)}, u32[]{:S(2)}) collective-permute-start(bf16[8,384,128]{2,1,0:T(8,128)(2,1)S(1)} %all_to_all.11.mine_hbm), channel_id=1, source_target_pairs={{0,1},{1,0},{2,3},{3,2},{4,5},{5,4},{6,7},{7,6},{8,9},{9,8},{10,11... | collective-permute-start | bytes 2359304 | tf_op jit(solution)/shard_map/ppermute | solution.py:199

commit v3 on v2

v3 whole, which is shorter than its diff:
```python
import functools

import jax
import jax.numpy as jnp
from jax import lax
from jax.experimental import pallas as pl
from jax.experimental.pallas import tpu as pltpu
from jax.sharding import PartitionSpec as P

F32, BF16 = jnp.float32, jnp.bfloat16
ROWS = 8
SPAN = 8
GROUP = 2
GRANT = 8


def twice(x):
    return jnp.concatenate([x, x], axis=-1)


def project(p_ref, a_ref, pa_ref, near_ref, acc_ref):
    fine, width = p_ref.shape[0], p_ref.shape[1]
    steps, clear = fine // ROWS, acc_ref.shape[0] // fine

    def step(g, _):
        for r in range(ROWS):
            i = g * ROWS + r
            left = p_ref[i].T
            for k in range(a_ref.shape[1]):
                pa_ref[i, k] = jnp.dot(left, a_ref[i, k], preferred_element_type=F32).astype(BF16)
            near_ref[fine + i] = twice(p_ref[i])
            at = pl.ds(pl.multiple_of(i * clear, width), clear)
            acc_ref[at, :] = jnp.zeros((clear, 2 * width), F32)
        return 0

    lax.fori_loop(0, steps, step, 0)


def galerkin(cols, tiles, pa, before_ref, after_ref, near_in, acc_in, keep_ref, send_ref, near, acc):
    fine, per_row, width = pa.shape[0], pa.shape[1], pa.shape[2]
    half, n_tiles = fine // 2, acc.shape[0] // width

    def fill(r, _):
        for start, ref in ((0, before_ref), (2 * fine, after_ref)):
            both = ref[r]
            near[start + r] = twice(both[:, :width])
            near[start + half + r] = twice(both[:, width:])
        return 0

    lax.fori_loop(0, half, fill, 0, unroll=4)

    def add(i, group, terms):
        ids = [tiles[k, i] for k in group]
        at = [pl.ds(pl.multiple_of(t * width, width), width) for t in ids]
        found, sums = [acc[rows, :] for rows in at], []
        for n, term in enumerate(terms):
            base = found[n]
            for m in range(n):
                base = jnp.where(ids[m] == ids[n], sums[m], base)
            sums.append(base + term)
        for rows, value in zip(at, sums):
            acc[rows, :] = value

    def step(g, _):
        for r in range(SPAN):
            i = g * SPAN + r
            terms = [
                jnp.dot(pa[i, k], near[cols[k, i]], preferred_element_type=F32) for k in range(per_row)
            ]
            for k in range(0, per_row, GROUP):
                add(i, range(k, k + GROUP), terms[k : k + GROUP])
        return 0

    lax.fori_loop(0, fine // SPAN, step, 0)

    first_core = lax.broadcasted_iota(jnp.int32, (8, 2 * width), 0) * 0 + lax.axis_index("sub") % 2 == 0
    left_half = lax.broadcasted_iota(jnp.int32, (8, 2 * width), 1) < width
    upper = lax.broadcasted_iota(jnp.int32, (8, 2 * width), 0) < 4
    groups, quads = keep_ref.shape[0], n_tiles // 4

    def pack(u, _):
        for y in range(groups):
            rows = []
            for w in range(2):

                def tile(q):
                    start = (2 * u + w + q * quads) * width + 8 * y
                    return acc[pl.ds(pl.multiple_of(start, 8), 8), :]

                even = jnp.where(left_half, tile(0), tile(2))
                odd = jnp.where(left_half, tile(1), tile(3))
                top = jnp.where(upper, even, pltpu.roll(odd, 4, 0))
                bottom = jnp.where(upper, pltpu.roll(even, 4, 0), odd)
                rows.append((jnp.where(first_core, top, bottom), jnp.where(first_core, bottom, top)))
            at = pl.ds(pl.multiple_of(16 * u, 16), 16)
            keep_ref[y, at, :] = jnp.concatenate([rows[0][0], rows[1][0]], axis=0)
            send_ref[y, at, :] = jnp.concatenate([rows[0][1], rows[1][1]], axis=0).astype(BF16)
        return 0

    lax.fori_loop(0, quads // 2, pack, 0, unroll=2)


def finish(got_ref, out_ref, total):
    peers, packed, lanes = got_ref.shape
    half, quads = lanes // 2, packed // 8
    n_tiles = 4 * quads
    sums = got_ref[0].astype(F32)
    for y in range(1, peers):
        sums = sums + got_ref[y].astype(F32)
    total[...] = sums
    slab = []
    for r in range(4):
        rows = [total[pl.ds(4 * s + r, quads, stride=8), :] for s in range(2)]
        turned = jnp.concatenate(rows, axis=0).T
        slab.append(jnp.concatenate([turned[:half], turned[half:]], axis=1))
    slab = jnp.concatenate(slab, axis=0)
    rest = jnp.concatenate([slab[:lanes, lanes:], slab[lanes:, lanes:]], axis=1)
    block = jnp.concatenate([slab[:, :lanes], rest], axis=0).astype(BF16)
    for y in range(peers):
        out_ref[y] = block


def spread(mine, other, out_hbm, out, sems):
    core = lax.axis_index("sub") % 2
    chips, packed, lanes = mine.shape
    slab, half = out.shape[0] // (2 * chips), lanes // 2

    def put(y):
        rows = pl.ds(2 * slab * y, 2 * slab)
        return pltpu.make_async_copy(out.at[rows], out_hbm.at[rows], sems.at[y])

    for y in range(chips):
        for ref, at in ((mine, core), (other, 1 - core)):
            start = pl.multiple_of((2 * y + at) * slab, slab)
            out[pl.ds(start, slab), 0:lanes] = ref[y, 0:slab, :]
            rest = ref[y, slab:packed, :]
            out[pl.ds(start, lanes), lanes : lanes + half] = rest[:, :half]
            out[pl.ds(start + lanes, lanes), lanes : lanes + half] = rest[:, half:]
        put(y).start()
    for y in range(chips):
        put(y).wait()


def body(n_tiles, a_blocks, p_blocks, a_cols, tile_of_item):
    fine, per_row, width = a_blocks.shape[1], a_blocks.shape[2], a_blocks.shape[3]
    subs, doms = lax.axis_size("sub"), lax.axis_size("dom")
    chips = subs // 2
    lanes = 2 * width
    half = fine // 2
    own = p_blocks[0]
    cols, tiles = a_cols[0].T, tile_of_item[0].T

    up = [(d, d + 1) for d in range(doms - 1)]
    down = [(d + 1, d) for d in range(doms - 1)]
    swap = [(s, s ^ 1) for s in range(subs)]
    columns = [[2 * y + c for y in range(chips)] for c in range(2)]

    packed = jnp.concatenate([own[:half], own[half:]], axis=-1)
    before = lax.ppermute(packed, "dom", up)
    after = lax.ppermute(packed, "dom", down)

    smem = pl.BlockSpec(memory_space=pltpu.SMEM)
    vmem = pl.BlockSpec(memory_space=pltpu.VMEM)
    anywhere = pl.BlockSpec(memory_space=pl.ANY)
    blocks = jax.ShapeDtypeStruct((fine, per_row, width, width), BF16)
    near = jax.ShapeDtypeStruct((3 * fine, width, lanes), BF16)
    sums = jax.ShapeDtypeStruct((n_tiles * width, lanes), F32)
    projected, own_near, clear = pl.pallas_call(
        project,
        out_shape=(blocks, near, sums),
        in_specs=[vmem, vmem],
        out_specs=(vmem, vmem, vmem),
        compiler_params=pltpu.CompilerParams(vmem_limit_bytes=GRANT << 20),
        cost_estimate=pl.CostEstimate(
            flops=fine * per_row * 2 * lanes**3, bytes_accessed=4 * a_blocks.size, transcendentals=0
        ),
        name="project",
    )(own, a_blocks[0])

    share = width // subs // 2 * n_tiles
    keep, send, _, _ = pl.pallas_call(
        galerkin,
        out_shape=(
            jax.ShapeDtypeStruct((chips, share, lanes), F32),
            jax.ShapeDtypeStruct((chips, share, lanes), BF16),
            near,
            sums,
        ),
        in_specs=[smem, smem, vmem, vmem, vmem, vmem, vmem],
        out_specs=(vmem, vmem, vmem, vmem),
        input_output_aliases={5: 2, 6: 3},
        compiler_params=pltpu.CompilerParams(vmem_limit_bytes=GRANT << 20),
        name="galerkin",
    )(cols, tiles, projected, before, after, own_near, clear)

    other = lax.ppermute(send, "sub", swap)
    merged = (keep + other.astype(F32)).astype(BF16)
    got = lax.all_to_all(merged, "sub", 0, 0, axis_index_groups=columns, tiled=True)
    block = pl.pallas_call(
        finish,
        out_shape=jax.ShapeDtypeStruct((chips, share, lanes), BF16),
        scratch_shapes=[pltpu.VMEM((share, lanes), F32)],
        compiler_params=pltpu.CompilerParams(vmem_limit_bytes=8 << 20),
        name="finish",
    )(got)
    mine = lax.all_to_all(block, "sub", 0, 0, axis_index_groups=columns, tiled=True)
    theirs = lax.ppermute(mine, "sub", swap)
    out = pl.pallas_call(
        spread,
        out_shape=jax.ShapeDtypeStruct((width * width, n_tiles), BF16),
        in_specs=[vmem, vmem],
        out_specs=anywhere,
        scratch_shapes=[pltpu.VMEM((width * width, n_tiles), BF16), pltpu.SemaphoreType.DMA((chips,))],
        compiler_params=pltpu.CompilerParams(vmem_limit_bytes=8 << 20),
        name="spread",
    )(mine, theirs)
    return out.reshape(width, width, n_tiles).transpose(2, 0, 1)[None]


def solution(mesh):
    placed = (
        P("dom", "sub", None, None, None),
        P("dom", "sub", None, None),
        P("dom", "sub", None),
        P("dom", "sub", None),
    )
    n_tiles = 12 * mesh.shape["sub"]
    return jax.shard_map(
        functools.partial(body, n_tiles),
        mesh=mesh,
        in_specs=placed,
        out_specs=P("dom", None, None, None),
        check_vma=False,
    )
```

time: 119 us -> 106 us (0.89)
  Pallas kernels: 17.6 us -> 9.32 us
  waiting for transfers between devices: 17 us -> 11.1 us
  local copies, waits for them, and re-layouts: 1.93 us -> 4.03 us
  other arithmetic: 1.83 us -> 0.42 us
    pallas_call x1, Pallas kernels: 12.9 us -> 4.67 us  [body(): pl.pallas_call(galerkin, out_shape=(jax.ShapeDtypeStruct((chips, share, l...]
    ppermute x1, waiting for transfers between devices: 5.84 us -> 0.21 us  [body(): after = lax.ppermute(packed, 'dom', down)]
    pallas_call x1, Pallas kernels: 4.36 us -> 1.47 us  [body(): pl.pallas_call(spread, out_shape=jax.ShapeDtypeStruct((width * width, n_t...]
    pallas_call x0 -> x1, Pallas kernels: none -> 2.83 us  [body(): pl.pallas_call(project, out_shape=(blocks, near, sums), in_specs=[vmem, v...]
    unnamed x4 -> x8, local copies, waits for them, and re-layouts: 0.76 us -> 2.79 us
    convert_element_type x1, other arithmetic: 1.61 us -> 0.2 us  [body(): merged = (keep + other.astype(F32)).astype(BF16)]
  transfers between devices with their start and end apart: 4 -> 4, of which waited for: 4 -> 4; matrix products, arithmetic and copies ran while one was open for 0% -> 0% of each run, Pallas kernels for 0% -> 3%
where the time goes in v3:
time: 106 us; the launch traced here: 105 us
  blocking collectives  52.6 us (50%)
  starting transfers between devices  27.9 us (26%)
  waiting for transfers between devices  11.1 us (10%)
  Pallas kernels  9.32 us (9%)
  local copies, waits for them, and re-layouts  4.03 us (4%)
    all_to_all x1, blocking collectives, body(): lax.all_to_all(merged, 'sub', 0, 0, axis_index_groups=columns, tiled=True)  29.4 us
    all_to_all x1, blocking collectives, body(): lax.all_to_all(block, 'sub', 0, 0, axis_index_groups=columns, tiled=True)  23.1 us
    ppermute x1, starting transfers between devices, body(): after = lax.ppermute(packed, 'dom', down)  17 us
    ppermute x1, waiting for transfers between devices, body(): before = lax.ppermute(packed, 'dom', up)  7.16 us
    ppermute x1, starting transfers between devices, body(): theirs = lax.ppermute(mine, 'sub', swap)  5.23 us
    pallas_call x1, Pallas kernels, body(): pl.pallas_call(galerkin, out_shape=(jax.ShapeDtypeStruct((chips, share, l...  4.67 us
    ppermute x1, starting transfers between devices, body(): other = lax.ppermute(send, 'sub', swap)  3.72 us
    pallas_call x1, Pallas kernels, body(): pl.pallas_call(project, out_shape=(blocks, near, sums), in_specs=[vmem, v...  2.83 us
  transfers between devices with their start and end apart: 4, of which 4 were waited for; matrix products, arithmetic and copies ran while one was open for 0% of the time, Pallas kernels for 3%

profile of v3, /device:TPU:9, one launch (start us, length us, event | category | flops | bytes accessed | tf_op | source)
XLA Modules:
  0.0 105.4 jit_solution(14894474340384477870)
XLA Ops:
  0.0 0.0 copy-start.1
  0.0 1.2 %slice_bitcast_fusion.1 = (bf16[24,64,64]{2,1,0:T(8,128)(2,1)S(1)}, bf16[24,64,64]{2,1,0:T(8,128)(2,1)S(1)}) fusion(bf16[1,48,64,64]{3,2,1,0:T(8,128)(2,1)} %param.5), kind=kLoop, calls=%fused_computation.3 | loop fusion | bytes 786432 | tf_op jit(solution)/shard_map/slice | solution.py:158
  1.2 0.2 pad_maximum_fusion
  1.5 17.0 %collective-permute-start.1 = (bf16[24,64,128]{2,1,0:T(8,128)(2,1)S(1)}, bf16[24,64,128]{2,1,0:T(8,128)(2,1)S(1)}, u32[]{:S(2)}, u32[]{:S(2)}) collective-permute-start(bf16[24,64,128]{2,1,0:T(8,128)(2,1)S(1)} %pad_maximum_fusion), channel_id=1, source_target_pairs={{16,0},{32,16},{48,32},{64,48},{80,64},{96,80},{112,96},{128,112},... | collective-permute-start | bytes 1179656 | tf_op jit(solution)/shard_map/ppermute | solution.py:160
  18.5 1.9 %collective-permute-start = (bf16[24,64,128]{2,1,0:T(8,128)(2,1)S(1)}, bf16[24,64,128]{2,1,0:T(8,128)(2,1)S(1)}, u32[]{:S(2)}, u32[]{:S(2)}) collective-permute-start(bf16[24,64,128]{2,1,0:T(8,128)(2,1)S(1)} %pad_maximum_fusion), channel_id=1, source_target_pairs={{0,16},{16,32},{32,48},{48,64},{64,80},{80,96},{96,112},{112,128},... | collective-permute-start | bytes 1179656 | tf_op jit(solution)/shard_map/ppermute | solution.py:159
  20.4 0.0 copy-done.1
  20.4 0.0 copy-start
  20.4 2.8 %copy-done = bf16[1,48,8,64,64]{4,3,2,1,0:T(8,128)(2,1)S(1)} copy-done((bf16[1,48,8,64,64]{4,3,2,1,0:T(8,128)(2,1)S(1)}, bf16[1,48,8,64,64]{4,3,2,1,0:T(8,128)(2,1)}, u32[]{:S(2)}) %copy-start) | copy-done | bytes 3145752
  23.2 0.0 copy-start.2
  23.2 0.0 copy-start.3
  23.2 2.8 %project.1 = (bf16[48,8,64,64]{3,2,1,0:T(8,128)(2,1)S(1)}, bf16[144,64,128]{2,1,0:T(8,128)(2,1)S(1)}, f32[12288,128]{1,0:T(8,128)S(1)}) custom-call(bf16[48,64,64]{2,1,0:T(8,128)(2,1)S(1)} %bitcast.18, bf16[48,8,64,64]{3,2,1,0:T(8,128)(2,1)S(1)} %bitcast.17), custom_call_target="tpu_custom_call" | custom-call | flops 1610612736 | bytes 6291456 | tf_op jit(solution)/shard_map/project/pallas_call | solution.py:168
  26.1 0.2 collective-permute-done.1.after_ref
  26.3 7.2 %collective-permute-done.before_ref = bf16[24,64,128]{2,1,0:T(8,128)(2,1)S(1)} collective-permute-done((bf16[24,64,128]{2,1,0:T(8,128)(2,1)S(1)}, bf16[24,64,128]{2,1,0:T(8,128)(2,1)S(1)}, u32[]{:S(2)}, u32[]{:S(2)}) %collective-permute-start) | collective-permute-done | bytes 393248 | tf_op jit(solution)/shard_map/ppermute | solution.py:159
  33.4 0.0 copy-done.2
  33.4 0.0 copy-done.3
  33.4 4.7 %galerkin.1 = (f32[8,384,128]{2,1,0:T(8,128)S(1)}, bf16[8,384,128]{2,1,0:T(8,128)(2,1)S(1)}, bf16[144,64,128]{2,1,0:T(8,128)(2,1)S(1)}, f32[12288,128]{1,0:T(8,128)S(1)}) custom-call(s32[8,48]{1,0:T(8,128)S(1)} %bitcast.19, s32[8,48]{1,0:T(8,128)S(1)} %bitcast.20, ...), custom_call_target="tpu_custom_call", output_to_operand_aliasing={{2}: (5, {}), {3}: (6, {})} | custom-call | tf_op jit(solution)/shard_map/galerkin/pallas_call | solution.py:181
  38.1 3.7 %collective-permute-start.2 = (bf16[8,384,128]{2,1,0:T(8,128)(2,1)S(1)}, bf16[8,384,128]{2,1,0:T(8,128)(2,1)S(1)}, u32[]{:S(2)}, u32[]{:S(2)}) collective-permute-start(bf16[8,384,128]{2,1,0:T(8,128)(2,1)S(1)} %get-tuple-element.14), channel_id=1, source_target_pairs={{0,1},{1,0},{2,3},{3,2},{4,5},{5,4},{6,7},{7,6},{8,9},{9,8},{10,11... | collective-permute-start | bytes 2359304 | tf_op jit(solution)/shard_map/ppermute | solution.py:196
  41.8 1.9 %collective-permute-done.2 = bf16[8,384,128]{2,1,0:T(8,128)(2,1)S(1)} collective-permute-done((bf16[8,384,128]{2,1,0:T(8,128)(2,1)S(1)}, bf16[8,384,128]{2,1,0:T(8,128)(2,1)S(1)}, u32[]{:S(2)}, u32[]{:S(2)}) %collective-permute-start.2) | collective-permute-done | bytes 786464 | tf_op jit(solution)/shard_map/ppermute | solution.py:196
  43.7 0.2 add_convert_fusion
  43.9 29.4 %all_to_all.10.got_ref = bf16[8,384,128]{2,1,0:T(8,128)(2,1)S(1)} all-to-all(bf16[8,384,128]{2,1,0:T(8,128)(2,1)S(1)} %add_convert_fusion), channel_id=1, replica_groups={{0,2,4,6,8,10,12,14},{1,3,5,7,9,11,13,15},{16,18,20,22,24,26,28,30},{17..., dimensions={0} | all-to-all | bytes 1572864 | tf_op jit(solution)/shard_map/all_to_all | solution.py:198
  73.3 0.4 finish.1
  73.7 23.1 %all_to_all.11.mine = bf16[8,384,128]{2,1,0:T(8,128)(2,1)S(1)} all-to-all(bf16[8,384,128]{2,1,0:T(8,128)(2,1)S(1)} %finish.1), channel_id=1, replica_groups={{0,2,4,6,8,10,12,14},{1,3,5,7,9,11,13,15},{16,18,20,22,24,26,28,30},{17..., dimensions={0} | all-to-all | bytes 1572864 | tf_op jit(solution)/shard_map/all_to_all | solution.py:206
  96.8 5.2 %collective-permute-start.3 = (bf16[8,384,128]{2,1,0:T(8,128)(2,1)S(1)}, bf16[8,384,128]{2,1,0:T(8,128)(2,1)S(1)}, u32[]{:S(2)}, u32[]{:S(2)}) collective-permute-start(bf16[8,384,128]{2,1,0:T(8,128)(2,1)S(1)} %all_to_all.11.mine), channel_id=1, source_target_pairs={{0,1},{1,0},{2,3},{3,2},{4,5},{5,4},{6,7},{7,6},{8,9},{9,8},{10,11... | collective-permute-start | bytes 2359304 | tf_op jit(solution)/shard_map/ppermute | solution.py:207
  102.1 1.9 %collective-permute-done.3.other = bf16[8,384,128]{2,1,0:T(8,128)(2,1)S(1)} collective-permute-done((bf16[8,384,128]{2,1,0:T(8,128)(2,1)S(1)}, bf16[8,384,128]{2,1,0:T(8,128)(2,1)S(1)}, u32[]{:S(2)}, u32[]{:S(2)}) %collective-permute-start.3) | collective-permute-done | bytes 786464 | tf_op jit(solution)/shard_map/ppermute | solution.py:207
  104.0 1.5 %spread.1 = bf16[4096,192]{1,0:T(8,128)(2,1)} custom-call(bf16[8,384,128]{2,1,0:T(8,128)(2,1)S(1)} %all_to_all.11.mine, bf16[8,384,128]{2,1,0:T(8,128)(2,1)S(1)} %collective-permute-done.3.other), custom_call_target="tpu_custom_call" | custom-call | tf_op jit(solution)/shard_map/spread/pallas_call | solution.py:208
Async XLA Ops:
  0.0 20.4 %copy-start.1 = (bf16[1,48,64,64]{3,2,1,0:T(8,128)(2,1)S(1)}, bf16[1,48,64,64]{3,2,1,0:T(8,128)(2,1)}, u32[]{:S(2)}) copy-start(bf16[1,48,64,64]{3,2,1,0:T(8,128)(2,1)} %param.5) | copy-start | bytes 1179652
  1.5 24.8 %collective-permute-start.1 = (bf16[24,64,128]{2,1,0:T(8,128)(2,1)S(1)}, bf16[24,64,128]{2,1,0:T(8,128)(2,1)S(1)}, u32[]{:S(2)}, u32[]{:S(2)}) collective-permute-start(bf16[24,64,128]{2,1,0:T(8,128)(2,1)S(1)} %pad_maximum_fusion), channel_id=1, source_target_pairs={{16,0},{32,16},{48,32},{64,48},{80,64},{96,80},{112,96},{128,112},... | collective-permute-start | bytes 1179656 | tf_op jit(solution)/shard_map/ppermute | solution.py:160
  18.5 14.9 %collective-permute-start = (bf16[24,64,128]{2,1,0:T(8,128)(2,1)S(1)}, bf16[24,64,128]{2,1,0:T(8,128)(2,1)S(1)}, u32[]{:S(2)}, u32[]{:S(2)}) collective-permute-start(bf16[24,64,128]{2,1,0:T(8,128)(2,1)S(1)} %pad_maximum_fusion), channel_id=1, source_target_pairs={{0,16},{16,32},{32,48},{48,64},{64,80},{80,96},{96,112},{112,128},... | collective-permute-start | bytes 1179656 | tf_op jit(solution)/shard_map/ppermute | solution.py:159
  20.4 2.8 %copy-start = (bf16[1,48,8,64,64]{4,3,2,1,0:T(8,128)(2,1)S(1)}, bf16[1,48,8,64,64]{4,3,2,1,0:T(8,128)(2,1)}, u32[]{:S(2)}) copy-start(bf16[1,48,8,64,64]{4,3,2,1,0:T(8,128)(2,1)} %param.4) | copy-start | bytes 9437188
  23.2 10.2 %copy-start.2 = (s32[1,48,8]{1,2,0:T(8,128)S(1)}, s32[1,48,8]{1,2,0:T(8,128)}, u32[]{:S(2)}) copy-start(s32[1,48,8]{1,2,0:T(8,128)} %param.6) | copy-start | bytes 4612
  23.2 10.2 %copy-start.3 = (s32[1,48,8]{1,2,0:T(8,128)S(1)}, s32[1,48,8]{1,2,0:T(8,128)}, u32[]{:S(2)}) copy-start(s32[1,48,8]{1,2,0:T(8,128)} %param.7) | copy-start | bytes 4612
  38.1 5.6 %collective-permute-start.2 = (bf16[8,384,128]{2,1,0:T(8,128)(2,1)S(1)}, bf16[8,384,128]{2,1,0:T(8,128)(2,1)S(1)}, u32[]{:S(2)}, u32[]{:S(2)}) collective-permute-start(bf16[8,384,128]{2,1,0:T(8,128)(2,1)S(1)} %get-tuple-element.14), channel_id=1, source_target_pairs={{0,1},{1,0},{2,3},{3,2},{4,5},{5,4},{6,7},{7,6},{8,9},{9,8},{10,11... | collective-permute-start | bytes 2359304 | tf_op jit(solution)/shard_map/ppermute | solution.py:196
  96.8 7.1 %collective-permute-start.3 = (bf16[8,384,128]{2,1,0:T(8,128)(2,1)S(1)}, bf16[8,384,128]{2,1,0:T(8,128)(2,1)S(1)}, u32[]{:S(2)}, u32[]{:S(2)}) collective-permute-start(bf16[8,384,128]{2,1,0:T(8,128)(2,1)S(1)} %all_to_all.11.mine), channel_id=1, source_target_pairs={{0,1},{1,0},{2,3},{3,2},{4,5},{5,4},{6,7},{7,6},{8,9},{9,8},{10,11... | collective-permute-start | bytes 2359304 | tf_op jit(solution)/shard_map/ppermute | solution.py:207

commit v4 on v3

--- a/solution.py
+++ b/solution.py
@@ -36,12 +36,14 @@
     lax.fori_loop(0, steps, step, 0)
 
 
-def galerkin(cols, tiles, pa, before_ref, after_ref, near_in, acc_in, keep_ref, send_ref, near, acc):
+def galerkin(cols, tiles, pa, pair_ref, cross_ref, near_in, acc_in, keep_ref, send_ref, near, acc):
     fine, per_row, width = pa.shape[0], pa.shape[1], pa.shape[2]
     half, n_tiles = fine // 2, acc.shape[0] // width
 
+    after = 2 * fine * (lax.axis_index("dom") % 2)
+
     def fill(r, _):
-        for start, ref in ((0, before_ref), (2 * fine, after_ref)):
+        for start, ref in ((2 * fine - after, pair_ref), (after, cross_ref)):
             both = ref[r]
             near[start + r] = twice(both[:, :width])
             near[start + half + r] = twice(both[:, width:])
@@ -150,14 +152,14 @@
     own = p_blocks[0]
     cols, tiles = a_cols[0].T, tile_of_item[0].T
 
-    up = [(d, d + 1) for d in range(doms - 1)]
-    down = [(d + 1, d) for d in range(doms - 1)]
+    pairs = [(d, d ^ 1) for d in range(doms)]
+    crossed = [(d, d + 1 if d % 2 else d - 1) for d in range(1, doms - 1)]
     swap = [(s, s ^ 1) for s in range(subs)]
     columns = [[2 * y + c for y in range(chips)] for c in range(2)]
 
     packed = jnp.concatenate([own[:half], own[half:]], axis=-1)
-    before = lax.ppermute(packed, "dom", up)
-    after = lax.ppermute(packed, "dom", down)
+    pair = lax.ppermute(packed, "dom", pairs)
+    cross = lax.ppermute(packed, "dom", crossed)
 
     smem = pl.BlockSpec(memory_space=pltpu.SMEM)
     vmem = pl.BlockSpec(memory_space=pltpu.VMEM)
@@ -191,7 +193,7 @@
         input_output_aliases={5: 2, 6: 3},
         compiler_params=pltpu.CompilerParams(vmem_limit_bytes=GRANT << 20),
         name="galerkin",
-    )(cols, tiles, projected, before, after, own_near, clear)
+    )(cols, tiles, projected, pair, cross, own_near, clear)
 
     other = lax.ppermute(send, "sub", swap)
     merged = (keep + other.astype(F32)).astype(BF16)

time: 106 us -> 103 us (0.972)
  the two profiles are of different devices: /device:TPU:9 before, /device:TPU:13 now
where the time goes in v4:
time: 103 us
  blocking collectives  52.6 us (51%)
  starting transfers between devices  28.8 us (28%)
  Pallas kernels  9.35 us (9%)
  waiting for transfers between devices  7.83 us (8%)
  local copies, waits for them, and re-layouts  4.03 us (4%)
    all_to_all x1, blocking collectives, body(): lax.all_to_all(merged, 'sub', 0, 0, axis_index_groups=columns, tiled=True)  29.4 us
    all_to_all x1, blocking collectives, body(): lax.all_to_all(block, 'sub', 0, 0, axis_index_groups=columns, tiled=True)  23.1 us
    ppermute x1, starting transfers between devices, body(): cross = lax.ppermute(packed, 'dom', crossed)  17.9 us
    ppermute x1, starting transfers between devices, body(): theirs = lax.ppermute(mine, 'sub', swap)  5.23 us
    pallas_call x1, Pallas kernels, body(): pl.pallas_call(galerkin, out_shape=(jax.ShapeDtypeStruct((chips, share, l...  4.69 us
    ppermute x1, starting transfers between devices, body(): other = lax.ppermute(send, 'sub', swap)  3.72 us
    pallas_call x1, Pallas kernels, body(): pl.pallas_call(project, out_shape=(blocks, near, sums), in_specs=[vmem, v...  2.83 us
    ppermute x1, waiting for transfers between devices, body(): pair = lax.ppermute(packed, 'dom', pairs)  2.81 us
  transfers between devices with their start and end apart: 4, of which 4 were waited for; matrix products, arithmetic and copies ran while one was open for 0% of the time, Pallas kernels for 3%

profile of v4, /device:TPU:13, one launch (start us, length us, event | category | flops | bytes accessed | tf_op | source)
XLA Modules:
  0.0 103.0 jit_solution(12073485646006239435)
XLA Ops:
  0.0 0.0 copy-start.1
  0.0 1.2 %slice_bitcast_fusion.1 = (bf16[24,64,64]{2,1,0:T(8,128)(2,1)S(1)}, bf16[24,64,64]{2,1,0:T(8,128)(2,1)S(1)}) fusion(bf16[1,48,64,64]{3,2,1,0:T(8,128)(2,1)} %param.5), kind=kLoop, calls=%fused_computation.3 | loop fusion | bytes 786432 | tf_op jit(solution)/shard_map/slice | solution.py:160
  1.2 0.2 pad_maximum_fusion
  1.5 17.9 %collective-permute-start.1 = (bf16[24,64,128]{2,1,0:T(8,128)(2,1)S(1)}, bf16[24,64,128]{2,1,0:T(8,128)(2,1)S(1)}, u32[]{:S(2)}, u32[]{:S(2)}) collective-permute-start(bf16[24,64,128]{2,1,0:T(8,128)(2,1)S(1)} %pad_maximum_fusion), channel_id=1, source_target_pairs={{16,32},{32,16},{48,64},{64,48},{80,96},{96,80},{112,128},{128,112... | collective-permute-start | bytes 1179656 | tf_op jit(solution)/shard_map/ppermute | solution.py:162
  19.4 1.9 %collective-permute-start = (bf16[24,64,128]{2,1,0:T(8,128)(2,1)S(1)}, bf16[24,64,128]{2,1,0:T(8,128)(2,1)S(1)}, u32[]{:S(2)}, u32[]{:S(2)}) collective-permute-start(bf16[24,64,128]{2,1,0:T(8,128)(2,1)S(1)} %pad_maximum_fusion), channel_id=1, source_target_pairs={{0,16},{16,0},{32,48},{48,32},{64,80},{80,64},{96,112},{112,96},{1... | collective-permute-start | bytes 1179656 | tf_op jit(solution)/shard_map/ppermute | solution.py:161
  21.3 0.0 copy-done.1
  21.3 0.0 copy-start
  21.3 2.8 %copy-done = bf16[1,48,8,64,64]{4,3,2,1,0:T(8,128)(2,1)S(1)} copy-done((bf16[1,48,8,64,64]{4,3,2,1,0:T(8,128)(2,1)S(1)}, bf16[1,48,8,64,64]{4,3,2,1,0:T(8,128)(2,1)}, u32[]{:S(2)}) %copy-start) | copy-done | bytes 3145752
  24.1 0.0 copy-start.2
  24.1 0.0 copy-start.3
  24.1 2.8 %project.1 = (bf16[48,8,64,64]{3,2,1,0:T(8,128)(2,1)S(1)}, bf16[144,64,128]{2,1,0:T(8,128)(2,1)S(1)}, f32[12288,128]{1,0:T(8,128)S(1)}) custom-call(bf16[48,64,64]{2,1,0:T(8,128)(2,1)S(1)} %bitcast.18, bf16[48,8,64,64]{3,2,1,0:T(8,128)(2,1)S(1)} %bitcast.17), custom_call_target="tpu_custom_call" | custom-call | flops 1610612736 | bytes 6291456 | tf_op jit(solution)/shard_map/project/pallas_call | solution.py:170
  27.0 1.2 %collective-permute-done.1.cross_ref = bf16[24,64,128]{2,1,0:T(8,128)(2,1)S(1)} collective-permute-done((bf16[24,64,128]{2,1,0:T(8,128)(2,1)S(1)}, bf16[24,64,128]{2,1,0:T(8,128)(2,1)S(1)}, u32[]{:S(2)}, u32[]{:S(2)}) %collective-permute-start.1) | collective-permute-done | bytes 393248 | tf_op jit(solution)/shard_map/ppermute | solution.py:162
  28.2 2.8 %collective-permute-done.pair_ref = bf16[24,64,128]{2,1,0:T(8,128)(2,1)S(1)} collective-permute-done((bf16[24,64,128]{2,1,0:T(8,128)(2,1)S(1)}, bf16[24,64,128]{2,1,0:T(8,128)(2,1)S(1)}, u32[]{:S(2)}, u32[]{:S(2)}) %collective-permute-start) | collective-permute-done | bytes 393248 | tf_op jit(solution)/shard_map/ppermute | solution.py:161
  31.0 0.0 copy-done.2
  31.0 0.0 copy-done.3
  31.0 4.7 %galerkin.1 = (f32[8,384,128]{2,1,0:T(8,128)S(1)}, bf16[8,384,128]{2,1,0:T(8,128)(2,1)S(1)}, bf16[144,64,128]{2,1,0:T(8,128)(2,1)S(1)}, f32[12288,128]{1,0:T(8,128)S(1)}) custom-call(s32[8,48]{1,0:T(8,128)S(1)} %bitcast.19, s32[8,48]{1,0:T(8,128)S(1)} %bitcast.20, ...), custom_call_target="tpu_custom_call", output_to_operand_aliasing={{2}: (5, {}), {3}: (6, {})} | custom-call | tf_op jit(solution)/shard_map/galerkin/pallas_call | solution.py:183
  35.7 3.7 %collective-permute-start.2 = (bf16[8,384,128]{2,1,0:T(8,128)(2,1)S(1)}, bf16[8,384,128]{2,1,0:T(8,128)(2,1)S(1)}, u32[]{:S(2)}, u32[]{:S(2)}) collective-permute-start(bf16[8,384,128]{2,1,0:T(8,128)(2,1)S(1)} %get-tuple-element.14), channel_id=1, source_target_pairs={{0,1},{1,0},{2,3},{3,2},{4,5},{5,4},{6,7},{7,6},{8,9},{9,8},{10,11... | collective-permute-start | bytes 2359304 | tf_op jit(solution)/shard_map/ppermute | solution.py:198
  39.4 1.9 %collective-permute-done.2 = bf16[8,384,128]{2,1,0:T(8,128)(2,1)S(1)} collective-permute-done((bf16[8,384,128]{2,1,0:T(8,128)(2,1)S(1)}, bf16[8,384,128]{2,1,0:T(8,128)(2,1)S(1)}, u32[]{:S(2)}, u32[]{:S(2)}) %collective-permute-start.2) | collective-permute-done | bytes 786464 | tf_op jit(solution)/shard_map/ppermute | solution.py:198
  41.3 0.2 add_convert_fusion
  41.5 29.4 %all_to_all.10.got_ref = bf16[8,384,128]{2,1,0:T(8,128)(2,1)S(1)} all-to-all(bf16[8,384,128]{2,1,0:T(8,128)(2,1)S(1)} %add_convert_fusion), channel_id=1, replica_groups={{0,2,4,6,8,10,12,14},{1,3,5,7,9,11,13,15},{16,18,20,22,24,26,28,30},{17..., dimensions={0} | all-to-all | bytes 1572864 | tf_op jit(solution)/shard_map/all_to_all | solution.py:200
  70.9 0.4 finish.1
  71.3 23.1 %all_to_all.11.mine = bf16[8,384,128]{2,1,0:T(8,128)(2,1)S(1)} all-to-all(bf16[8,384,128]{2,1,0:T(8,128)(2,1)S(1)} %finish.1), channel_id=1, replica_groups={{0,2,4,6,8,10,12,14},{1,3,5,7,9,11,13,15},{16,18,20,22,24,26,28,30},{17..., dimensions={0} | all-to-all | bytes 1572864 | tf_op jit(solution)/shard_map/all_to_all | solution.py:208
  94.4 5.2 %collective-permute-start.3 = (bf16[8,384,128]{2,1,0:T(8,128)(2,1)S(1)}, bf16[8,384,128]{2,1,0:T(8,128)(2,1)S(1)}, u32[]{:S(2)}, u32[]{:S(2)}) collective-permute-start(bf16[8,384,128]{2,1,0:T(8,128)(2,1)S(1)} %all_to_all.11.mine), channel_id=1, source_target_pairs={{0,1},{1,0},{2,3},{3,2},{4,5},{5,4},{6,7},{7,6},{8,9},{9,8},{10,11... | collective-permute-start | bytes 2359304 | tf_op jit(solution)/shard_map/ppermute | solution.py:209
  99.7 1.9 %collective-permute-done.3.other = bf16[8,384,128]{2,1,0:T(8,128)(2,1)S(1)} collective-permute-done((bf16[8,384,128]{2,1,0:T(8,128)(2,1)S(1)}, bf16[8,384,128]{2,1,0:T(8,128)(2,1)S(1)}, u32[]{:S(2)}, u32[]{:S(2)}) %collective-permute-start.3) | collective-permute-done | bytes 786464 | tf_op jit(solution)/shard_map/ppermute | solution.py:209
  101.6 1.5 %spread.1 = bf16[4096,192]{1,0:T(8,128)(2,1)} custom-call(bf16[8,384,128]{2,1,0:T(8,128)(2,1)S(1)} %all_to_all.11.mine, bf16[8,384,128]{2,1,0:T(8,128)(2,1)S(1)} %collective-permute-done.3.other), custom_call_target="tpu_custom_call" | custom-call | tf_op jit(solution)/shard_map/spread/pallas_call | solution.py:210
Async XLA Ops:
  0.0 21.3 %copy-start.1 = (bf16[1,48,64,64]{3,2,1,0:T(8,128)(2,1)S(1)}, bf16[1,48,64,64]{3,2,1,0:T(8,128)(2,1)}, u32[]{:S(2)}) copy-start(bf16[1,48,64,64]{3,2,1,0:T(8,128)(2,1)} %param.5) | copy-start | bytes 1179652
  1.5 26.7 %collective-permute-start.1 = (bf16[24,64,128]{2,1,0:T(8,128)(2,1)S(1)}, bf16[24,64,128]{2,1,0:T(8,128)(2,1)S(1)}, u32[]{:S(2)}, u32[]{:S(2)}) collective-permute-start(bf16[24,64,128]{2,1,0:T(8,128)(2,1)S(1)} %pad_maximum_fusion), channel_id=1, source_target_pairs={{16,32},{32,16},{48,64},{64,48},{80,96},{96,80},{112,128},{128,112... | collective-permute-start | bytes 1179656 | tf_op jit(solution)/shard_map/ppermute | solution.py:162
  19.4 11.6 %collective-permute-start = (bf16[24,64,128]{2,1,0:T(8,128)(2,1)S(1)}, bf16[24,64,128]{2,1,0:T(8,128)(2,1)S(1)}, u32[]{:S(2)}, u32[]{:S(2)}) collective-permute-start(bf16[24,64,128]{2,1,0:T(8,128)(2,1)S(1)} %pad_maximum_fusion), channel_id=1, source_target_pairs={{0,16},{16,0},{32,48},{48,32},{64,80},{80,64},{96,112},{112,96},{1... | collective-permute-start | bytes 1179656 | tf_op jit(solution)/shard_map/ppermute | solution.py:161
  21.3 2.8 %copy-start = (bf16[1,48,8,64,64]{4,3,2,1,0:T(8,128)(2,1)S(1)}, bf16[1,48,8,64,64]{4,3,2,1,0:T(8,128)(2,1)}, u32[]{:S(2)}) copy-start(bf16[1,48,8,64,64]{4,3,2,1,0:T(8,128)(2,1)} %param.4) | copy-start | bytes 9437188
  24.1 6.9 %copy-start.2 = (s32[1,48,8]{1,2,0:T(8,128)S(1)}, s32[1,48,8]{1,2,0:T(8,128)}, u32[]{:S(2)}) copy-start(s32[1,48,8]{1,2,0:T(8,128)} %param.6) | copy-start | bytes 4612
  24.1 6.9 %copy-start.3 = (s32[1,48,8]{1,2,0:T(8,128)S(1)}, s32[1,48,8]{1,2,0:T(8,128)}, u32[]{:S(2)}) copy-start(s32[1,48,8]{1,2,0:T(8,128)} %param.7) | copy-start | bytes 4612
  35.7 5.6 %collective-permute-start.2 = (bf16[8,384,128]{2,1,0:T(8,128)(2,1)S(1)}, bf16[8,384,128]{2,1,0:T(8,128)(2,1)S(1)}, u32[]{:S(2)}, u32[]{:S(2)}) collective-permute-start(bf16[8,384,128]{2,1,0:T(8,128)(2,1)S(1)} %get-tuple-element.14), channel_id=1, source_target_pairs={{0,1},{1,0},{2,3},{3,2},{4,5},{5,4},{6,7},{7,6},{8,9},{9,8},{10,11... | collective-permute-start | bytes 2359304 | tf_op jit(solution)/shard_map/ppermute | solution.py:198
  94.4 7.1 %collective-permute-start.3 = (bf16[8,384,128]{2,1,0:T(8,128)(2,1)S(1)}, bf16[8,384,128]{2,1,0:T(8,128)(2,1)S(1)}, u32[]{:S(2)}, u32[]{:S(2)}) collective-permute-start(bf16[8,384,128]{2,1,0:T(8,128)(2,1)S(1)} %all_to_all.11.mine), channel_id=1, source_target_pairs={{0,1},{1,0},{2,3},{3,2},{4,5},{5,4},{6,7},{7,6},{8,9},{9,8},{10,11... | collective-permute-start | bytes 2359304 | tf_op jit(solution)/shard_map/ppermute | solution.py:209

commit v5 on v4

--- a/solution.py
+++ b/solution.py
@@ -7,10 +7,12 @@
 from jax.experimental.pallas import tpu as pltpu
 from jax.sharding import PartitionSpec as P
 
+
 F32, BF16 = jnp.float32, jnp.bfloat16
 ROWS = 8
 SPAN = 8
 GROUP = 2
+DEPTH = 8
 GRANT = 8
 
 
@@ -36,15 +38,15 @@
     lax.fori_loop(0, steps, step, 0)
 
 
-def galerkin(cols, tiles, pa, pair_ref, cross_ref, near_in, acc_in, keep_ref, send_ref, near, acc):
+def galerkin(cols, tiles, pa, early_ref, cross_ref, late_ref, near_in, acc_in, keep_ref, send_ref, near, acc):
     fine, per_row, width = pa.shape[0], pa.shape[1], pa.shape[2]
     half, n_tiles = fine // 2, acc.shape[0] // width
 
     after = 2 * fine * (lax.axis_index("dom") % 2)
 
     def fill(r, _):
-        for start, ref in ((2 * fine - after, pair_ref), (after, cross_ref)):
-            both = ref[r]
+        pair = early_ref[r] + late_ref[r]
+        for start, both in ((2 * fine - after, pair), (after, cross_ref[r])):
             near[start + r] = twice(both[:, :width])
             near[start + half + r] = twice(both[:, width:])
         return 0
@@ -105,7 +107,6 @@
 def finish(got_ref, out_ref, total):
     peers, packed, lanes = got_ref.shape
     half, quads = lanes // 2, packed // 8
-    n_tiles = 4 * quads
     sums = got_ref[0].astype(F32)
     for y in range(1, peers):
         sums = sums + got_ref[y].astype(F32)
@@ -152,14 +153,16 @@
     own = p_blocks[0]
     cols, tiles = a_cols[0].T, tile_of_item[0].T
 
-    pairs = [(d, d ^ 1) for d in range(doms)]
+    early = [(d, d ^ 1) for d in range(doms) if d % DEPTH < 2]
     crossed = [(d, d + 1 if d % 2 else d - 1) for d in range(1, doms - 1)]
+    late = [(d, d ^ 1) for d in range(doms) if d % DEPTH >= 2]
     swap = [(s, s ^ 1) for s in range(subs)]
     columns = [[2 * y + c for y in range(chips)] for c in range(2)]
 
     packed = jnp.concatenate([own[:half], own[half:]], axis=-1)
-    pair = lax.ppermute(packed, "dom", pairs)
+    early = lax.ppermute(packed, "dom", early)
     cross = lax.ppermute(packed, "dom", crossed)
+    late = lax.ppermute(packed, "dom", late)
 
     smem = pl.BlockSpec(memory_space=pltpu.SMEM)
     vmem = pl.BlockSpec(memory_space=pltpu.VMEM)
@@ -188,12 +191,12 @@
             near,
             sums,
         ),
-        in_specs=[smem, smem, vmem, vmem, vmem, vmem, vmem],
+        in_specs=[smem, smem] + [vmem] * 6,
         out_specs=(vmem, vmem, vmem, vmem),
-        input_output_aliases={5: 2, 6: 3},
+        input_output_aliases={6: 2, 7: 3},
         compiler_params=pltpu.CompilerParams(vmem_limit_bytes=GRANT << 20),
         name="galerkin",
-    )(cols, tiles, projected, pair, cross, own_near, clear)
+    )(cols, tiles, projected, early, cross, late, own_near, clear)
 
     other = lax.ppermute(send, "sub", swap)
     merged = (keep + other.astype(F32)).astype(BF16)

time: 103 us -> 105 us (1.019)
  starting transfers between devices: 28.8 us -> 30.7 us
    ppermute x1, starting transfers between devices: 17.9 us -> 19.1 us  [body(): cross = lax.ppermute(packed, 'dom', crossed)]
    ppermute x1 -> x2, starting transfers between devices: 1.92 us -> 2.61 us  [the longest x1 1.92 us: body(): early = lax.ppermute(packed, 'dom', early)]
    ppermute x1 -> x2, waiting for transfers between devices: 2.81 us -> 2.81 us  [the longest x1 2.81 us: body(): early = lax.ppermute(packed, 'dom', early)]
  transfers between devices with their start and end apart: 4 -> 5, of which waited for: 4 -> 4; matrix products, arithmetic and copies ran while one was open for 0% -> 0% of each run, Pallas kernels for 3% -> 3%
where the time goes in v5:
time: 105 us
  blocking collectives  52.6 us (50%)
  starting transfers between devices  30.7 us (29%)
  Pallas kernels  9.36 us (9%)
  waiting for transfers between devices  7.82 us (7%)
  local copies, waits for them, and re-layouts  4.03 us (4%)
    all_to_all x1, blocking collectives, body(): lax.all_to_all(merged, 'sub', 0, 0, axis_index_groups=columns, tiled=True)  29.4 us
    all_to_all x1, blocking collectives, body(): lax.all_to_all(block, 'sub', 0, 0, axis_index_groups=columns, tiled=True)  23.1 us
    ppermute x1, starting transfers between devices, body(): cross = lax.ppermute(packed, 'dom', crossed)  19.1 us
    ppermute x1, starting transfers between devices, body(): theirs = lax.ppermute(mine, 'sub', swap)  5.23 us
    pallas_call x1, Pallas kernels, body(): pl.pallas_call(galerkin, out_shape=(jax.ShapeDtypeStruct((chips, share, l...  4.71 us
    ppermute x1, starting transfers between devices, body(): other = lax.ppermute(send, 'sub', swap)  3.72 us
    pallas_call x1, Pallas kernels, body(): pl.pallas_call(project, out_shape=(blocks, near, sums), in_specs=[vmem, v...  2.83 us
    ppermute x1, waiting for transfers between devices, body(): early = lax.ppermute(packed, 'dom', early)  2.81 us
  transfers between devices with their start and end apart: 5, of which 4 were waited for; matrix products, arithmetic and copies ran while one was open for 0% of the time, Pallas kernels for 3%

profile of v5, /device:TPU:13, one launch (start us, length us, event | category | flops | bytes accessed | tf_op | source)
XLA Modules:
  0.0 105.0 jit_solution(14852849047777048261)
XLA Ops:
  0.0 0.0 copy-start.1
  0.0 1.2 %slice_bitcast_fusion.1 = (bf16[24,64,64]{2,1,0:T(8,128)(2,1)S(1)}, bf16[24,64,64]{2,1,0:T(8,128)(2,1)S(1)}) fusion(bf16[1,48,64,64]{3,2,1,0:T(8,128)(2,1)} %param.5), kind=kLoop, calls=%fused_computation.3 | loop fusion | bytes 786432 | tf_op jit(solution)/shard_map/slice | solution.py:162
  1.2 0.2 pad_maximum_fusion
  1.5 0.7 collective-permute-start.2
  2.2 19.1 %collective-permute-start.1 = (bf16[24,64,128]{2,1,0:T(8,128)(2,1)S(1)}, bf16[24,64,128]{2,1,0:T(8,128)(2,1)S(1)}, u32[]{:S(2)}, u32[]{:S(2)}) collective-permute-start(bf16[24,64,128]{2,1,0:T(8,128)(2,1)S(1)} %pad_maximum_fusion), channel_id=1, source_target_pairs={{16,32},{32,16},{48,64},{64,48},{80,96},{96,80},{112,128},{128,112... | collective-permute-start | bytes 1179656 | tf_op jit(solution)/shard_map/ppermute | solution.py:164
  21.3 1.9 %collective-permute-start = (bf16[24,64,128]{2,1,0:T(8,128)(2,1)S(1)}, bf16[24,64,128]{2,1,0:T(8,128)(2,1)S(1)}, u32[]{:S(2)}, u32[]{:S(2)}) collective-permute-start(bf16[24,64,128]{2,1,0:T(8,128)(2,1)S(1)} %pad_maximum_fusion), channel_id=1, source_target_pairs={{0,16},{16,0},{128,144},{144,128},{256,272},{272,256},{384,400},{4... | collective-permute-start | bytes 1179656 | tf_op jit(solution)/shard_map/ppermute | solution.py:163
  23.2 0.0 copy-done.1
  23.3 0.0 copy-start
  23.3 2.8 %copy-done = bf16[1,48,8,64,64]{4,3,2,1,0:T(8,128)(2,1)S(1)} copy-done((bf16[1,48,8,64,64]{4,3,2,1,0:T(8,128)(2,1)S(1)}, bf16[1,48,8,64,64]{4,3,2,1,0:T(8,128)(2,1)}, u32[]{:S(2)}) %copy-start) | copy-done | bytes 3145752
  26.0 0.0 copy-start.2
  26.0 0.0 copy-start.3
  26.0 2.8 %project.1 = (bf16[48,8,64,64]{3,2,1,0:T(8,128)(2,1)S(1)}, bf16[144,64,128]{2,1,0:T(8,128)(2,1)S(1)}, f32[12288,128]{1,0:T(8,128)S(1)}) custom-call(bf16[48,64,64]{2,1,0:T(8,128)(2,1)S(1)} %bitcast.18, bf16[48,8,64,64]{3,2,1,0:T(8,128)(2,1)S(1)} %bitcast.17), custom_call_target="tpu_custom_call" | custom-call | flops 1610612736 | bytes 6291456 | tf_op jit(solution)/shard_map/project/pallas_call | solution.py:173
  28.9 0.0 collective-permute-done.2.late_ref
  28.9 1.2 %collective-permute-done.1.cross_ref = bf16[24,64,128]{2,1,0:T(8,128)(2,1)S(1)} collective-permute-done((bf16[24,64,128]{2,1,0:T(8,128)(2,1)S(1)}, bf16[24,64,128]{2,1,0:T(8,128)(2,1)S(1)}, u32[]{:S(2)}, u32[]{:S(2)}) %collective-permute-start.1) | collective-permute-done | bytes 393248 | tf_op jit(solution)/shard_map/ppermute | solution.py:164
  30.1 2.8 %collective-permute-done.early_ref = bf16[24,64,128]{2,1,0:T(8,128)(2,1)S(1)} collective-permute-done((bf16[24,64,128]{2,1,0:T(8,128)(2,1)S(1)}, bf16[24,64,128]{2,1,0:T(8,128)(2,1)S(1)}, u32[]{:S(2)}, u32[]{:S(2)}) %collective-permute-start) | collective-permute-done | bytes 393248 | tf_op jit(solution)/shard_map/ppermute | solution.py:163
  32.9 0.0 copy-done.2
  32.9 0.0 copy-done.3
  32.9 4.7 %galerkin.1 = (f32[8,384,128]{2,1,0:T(8,128)S(1)}, bf16[8,384,128]{2,1,0:T(8,128)(2,1)S(1)}, bf16[144,64,128]{2,1,0:T(8,128)(2,1)S(1)}, f32[12288,128]{1,0:T(8,128)S(1)}) custom-call(s32[8,48]{1,0:T(8,128)S(1)} %bitcast.19, s32[8,48]{1,0:T(8,128)S(1)} %bitcast.20, ...), custom_call_target="tpu_custom_call", output_to_operand_aliasing={{2}: (6, {}), {3}: (7, {})} | custom-call | tf_op jit(solution)/shard_map/galerkin/pallas_call | solution.py:186
  37.7 3.7 %collective-permute-start.3 = (bf16[8,384,128]{2,1,0:T(8,128)(2,1)S(1)}, bf16[8,384,128]{2,1,0:T(8,128)(2,1)S(1)}, u32[]{:S(2)}, u32[]{:S(2)}) collective-permute-start(bf16[8,384,128]{2,1,0:T(8,128)(2,1)S(1)} %get-tuple-element.14), channel_id=1, source_target_pairs={{0,1},{1,0},{2,3},{3,2},{4,5},{5,4},{6,7},{7,6},{8,9},{9,8},{10,11... | collective-permute-start | bytes 2359304 | tf_op jit(solution)/shard_map/ppermute | solution.py:201
  41.4 1.9 %collective-permute-done.3 = bf16[8,384,128]{2,1,0:T(8,128)(2,1)S(1)} collective-permute-done((bf16[8,384,128]{2,1,0:T(8,128)(2,1)S(1)}, bf16[8,384,128]{2,1,0:T(8,128)(2,1)S(1)}, u32[]{:S(2)}, u32[]{:S(2)}) %collective-permute-start.3) | collective-permute-done | bytes 786464 | tf_op jit(solution)/shard_map/ppermute | solution.py:201
  43.3 0.2 add_convert_fusion
  43.5 29.4 %all_to_all.10.got_ref = bf16[8,384,128]{2,1,0:T(8,128)(2,1)S(1)} all-to-all(bf16[8,384,128]{2,1,0:T(8,128)(2,1)S(1)} %add_convert_fusion), channel_id=1, replica_groups={{0,2,4,6,8,10,12,14},{1,3,5,7,9,11,13,15},{16,18,20,22,24,26,28,30},{17..., dimensions={0} | all-to-all | bytes 1572864 | tf_op jit(solution)/shard_map/all_to_all | solution.py:203
  72.9 0.4 finish.1
  73.2 23.1 %all_to_all.11.mine = bf16[8,384,128]{2,1,0:T(8,128)(2,1)S(1)} all-to-all(bf16[8,384,128]{2,1,0:T(8,128)(2,1)S(1)} %finish.1), channel_id=1, replica_groups={{0,2,4,6,8,10,12,14},{1,3,5,7,9,11,13,15},{16,18,20,22,24,26,28,30},{17..., dimensions={0} | all-to-all | bytes 1572864 | tf_op jit(solution)/shard_map/all_to_all | solution.py:211
  96.4 5.2 %collective-permute-start.4 = (bf16[8,384,128]{2,1,0:T(8,128)(2,1)S(1)}, bf16[8,384,128]{2,1,0:T(8,128)(2,1)S(1)}, u32[]{:S(2)}, u32[]{:S(2)}) collective-permute-start(bf16[8,384,128]{2,1,0:T(8,128)(2,1)S(1)} %all_to_all.11.mine), channel_id=1, source_target_pairs={{0,1},{1,0},{2,3},{3,2},{4,5},{5,4},{6,7},{7,6},{8,9},{9,8},{10,11... | collective-permute-start | bytes 2359304 | tf_op jit(solution)/shard_map/ppermute | solution.py:212
  101.6 1.9 %collective-permute-done.4.other = bf16[8,384,128]{2,1,0:T(8,128)(2,1)S(1)} collective-permute-done((bf16[8,384,128]{2,1,0:T(8,128)(2,1)S(1)}, bf16[8,384,128]{2,1,0:T(8,128)(2,1)S(1)}, u32[]{:S(2)}, u32[]{:S(2)}) %collective-permute-start.4) | collective-permute-done | bytes 786464 | tf_op jit(solution)/shard_map/ppermute | solution.py:212
  103.5 1.5 %spread.1 = bf16[4096,192]{1,0:T(8,128)(2,1)} custom-call(bf16[8,384,128]{2,1,0:T(8,128)(2,1)S(1)} %all_to_all.11.mine, bf16[8,384,128]{2,1,0:T(8,128)(2,1)S(1)} %collective-permute-done.4.other), custom_call_target="tpu_custom_call" | custom-call | tf_op jit(solution)/shard_map/spread/pallas_call | solution.py:213
Async XLA Ops:
  0.0 23.2 %copy-start.1 = (bf16[1,48,64,64]{3,2,1,0:T(8,128)(2,1)S(1)}, bf16[1,48,64,64]{3,2,1,0:T(8,128)(2,1)}, u32[]{:S(2)}) copy-start(bf16[1,48,64,64]{3,2,1,0:T(8,128)(2,1)} %param.5) | copy-start | bytes 1179652
  1.5 27.4 %collective-permute-start.2 = (bf16[24,64,128]{2,1,0:T(8,128)(2,1)S(1)}, bf16[24,64,128]{2,1,0:T(8,128)(2,1)S(1)}, u32[]{:S(2)}, u32[]{:S(2)}) collective-permute-start(bf16[24,64,128]{2,1,0:T(8,128)(2,1)S(1)} %pad_maximum_fusion), channel_id=1, source_target_pairs={{32,48},{48,32},{64,80},{80,64},{96,112},{112,96},{160,176},{176,1... | collective-permute-start | bytes 1179656 | tf_op jit(solution)/shard_map/ppermute | solution.py:165
  2.2 28.0 %collective-permute-start.1 = (bf16[24,64,128]{2,1,0:T(8,128)(2,1)S(1)}, bf16[24,64,128]{2,1,0:T(8,128)(2,1)S(1)}, u32[]{:S(2)}, u32[]{:S(2)}) collective-permute-start(bf16[24,64,128]{2,1,0:T(8,128)(2,1)S(1)} %pad_maximum_fusion), channel_id=1, source_target_pairs={{16,32},{32,16},{48,64},{64,48},{80,96},{96,80},{112,128},{128,112... | collective-permute-start | bytes 1179656 | tf_op jit(solution)/shard_map/ppermute | solution.py:164
  21.3 11.6 %collective-permute-start = (bf16[24,64,128]{2,1,0:T(8,128)(2,1)S(1)}, bf16[24,64,128]{2,1,0:T(8,128)(2,1)S(1)}, u32[]{:S(2)}, u32[]{:S(2)}) collective-permute-start(bf16[24,64,128]{2,1,0:T(8,128)(2,1)S(1)} %pad_maximum_fusion), channel_id=1, source_target_pairs={{0,16},{16,0},{128,144},{144,128},{256,272},{272,256},{384,400},{4... | collective-permute-start | bytes 1179656 | tf_op jit(solution)/shard_map/ppermute | solution.py:163
  23.3 2.8 %copy-start = (bf16[1,48,8,64,64]{4,3,2,1,0:T(8,128)(2,1)S(1)}, bf16[1,48,8,64,64]{4,3,2,1,0:T(8,128)(2,1)}, u32[]{:S(2)}) copy-start(bf16[1,48,8,64,64]{4,3,2,1,0:T(8,128)(2,1)} %param.4) | copy-start | bytes 9437188
  26.0 6.9 %copy-start.2 = (s32[1,48,8]{1,2,0:T(8,128)S(1)}, s32[1,48,8]{1,2,0:T(8,128)}, u32[]{:S(2)}) copy-start(s32[1,48,8]{1,2,0:T(8,128)} %param.6) | copy-start | bytes 4612
  26.0 6.9 %copy-start.3 = (s32[1,48,8]{1,2,0:T(8,128)S(1)}, s32[1,48,8]{1,2,0:T(8,128)}, u32[]{:S(2)}) copy-start(s32[1,48,8]{1,2,0:T(8,128)} %param.7) | copy-start | bytes 4612
  37.7 5.6 %collective-permute-start.3 = (bf16[8,384,128]{2,1,0:T(8,128)(2,1)S(1)}, bf16[8,384,128]{2,1,0:T(8,128)(2,1)S(1)}, u32[]{:S(2)}, u32[]{:S(2)}) collective-permute-start(bf16[8,384,128]{2,1,0:T(8,128)(2,1)S(1)} %get-tuple-element.14), channel_id=1, source_target_pairs={{0,1},{1,0},{2,3},{3,2},{4,5},{5,4},{6,7},{7,6},{8,9},{9,8},{10,11... | collective-permute-start | bytes 2359304 | tf_op jit(solution)/shard_map/ppermute | solution.py:201
  96.4 7.1 %collective-permute-start.4 = (bf16[8,384,128]{2,1,0:T(8,128)(2,1)S(1)}, bf16[8,384,128]{2,1,0:T(8,128)(2,1)S(1)}, u32[]{:S(2)}, u32[]{:S(2)}) collective-permute-start(bf16[8,384,128]{2,1,0:T(8,128)(2,1)S(1)} %all_to_all.11.mine), channel_id=1, source_target_pairs={{0,1},{1,0},{2,3},{3,2},{4,5},{5,4},{6,7},{7,6},{8,9},{9,8},{10,11... | collective-permute-start | bytes 2359304 | tf_op jit(solution)/shard_map/ppermute | solution.py:212

commit v6 on v5

--- a/solution.py
+++ b/solution.py
@@ -123,8 +123,8 @@
         out_ref[y] = block
 
 
-def spread(mine, other, out_hbm, out, sems):
-    core = lax.axis_index("sub") % 2
+def spread(first, second, mine, other, out_hbm, out, sems):
+    core = lax.min(first[0], second[0])
     chips, packed, lanes = mine.shape
     slab, half = out.shape[0] // (2 * chips), lanes // 2
 
@@ -200,7 +200,12 @@
 
     other = lax.ppermute(send, "sub", swap)
     merged = (keep + other.astype(F32)).astype(BF16)
-    got = lax.all_to_all(merged, "sub", 0, 0, axis_index_groups=columns, tiled=True)
+    exchange = functools.partial(
+        lax.all_to_all, axis_name="sub", split_axis=0, concat_axis=0, axis_index_groups=columns, tiled=True
+    )
+    got = exchange(merged)
+    first = lax.axis_index("sub").reshape(1) % 2
+    second = lax.axis_index("sub").reshape(1) & 1
     block = pl.pallas_call(
         finish,
         out_shape=jax.ShapeDtypeStruct((chips, share, lanes), BF16),
@@ -208,17 +213,17 @@
         compiler_params=pltpu.CompilerParams(vmem_limit_bytes=8 << 20),
         name="finish",
     )(got)
-    mine = lax.all_to_all(block, "sub", 0, 0, axis_index_groups=columns, tiled=True)
+    mine = exchange(block)
     theirs = lax.ppermute(mine, "sub", swap)
     out = pl.pallas_call(
         spread,
         out_shape=jax.ShapeDtypeStruct((width * width, n_tiles), BF16),
-        in_specs=[vmem, vmem],
+        in_specs=[smem, smem, vmem, vmem],
         out_specs=anywhere,
         scratch_shapes=[pltpu.VMEM((width * width, n_tiles), BF16), pltpu.SemaphoreType.DMA((chips,))],
         compiler_params=pltpu.CompilerParams(vmem_limit_bytes=8 << 20),
         name="spread",
-    )(mine, theirs)
+    )(first, second, mine, theirs)
     return out.reshape(width, width, n_tiles).transpose(2, 0, 1)[None]
 
 

time: 105 us -> 105 us (level)
  no operation moved by 1% of the time
where the time goes in v6:
time: 105 us
  blocking collectives  52.6 us (50%)
  starting transfers between devices  30.7 us (29%)
  Pallas kernels  9.37 us (9%)
  waiting for transfers between devices  7.81 us (7%)
  local copies, waits for them, and re-layouts  4.03 us (4%)
    all_to_all x1, blocking collectives, body(): got = exchange(merged)  29.4 us
    all_to_all x1, blocking collectives, body(): mine = exchange(block)  23.1 us
    ppermute x1, starting transfers between devices, body(): cross = lax.ppermute(packed, 'dom', crossed)  19.1 us
    ppermute x1, starting transfers between devices, body(): theirs = lax.ppermute(mine, 'sub', swap)  5.23 us
    pallas_call x1, Pallas kernels, body(): pl.pallas_call(galerkin, out_shape=(jax.ShapeDtypeStruct((chips, share, l...  4.71 us
    ppermute x1, starting transfers between devices, body(): other = lax.ppermute(send, 'sub', swap)  3.72 us
    pallas_call x1, Pallas kernels, body(): pl.pallas_call(project, out_shape=(blocks, near, sums), in_specs=[vmem, v...  2.83 us
    ppermute x1, waiting for transfers between devices, body(): early = lax.ppermute(packed, 'dom', early)  2.81 us
  transfers between devices with their start and end apart: 5, of which 4 were waited for; matrix products, arithmetic and copies ran while one was open for 0% of the time, Pallas kernels for 3%

profile of v6, /device:TPU:13, one launch (start us, length us, event | category | flops | bytes accessed | tf_op | source)
XLA Modules:
  0.0 105.0 jit_solution(11504715348576857922)
XLA Ops:
  0.0 0.0 copy-start.1
  0.0 1.2 %slice_bitcast_fusion.1 = (bf16[24,64,64]{2,1,0:T(8,128)(2,1)S(1)}, bf16[24,64,64]{2,1,0:T(8,128)(2,1)S(1)}) fusion(bf16[1,48,64,64]{3,2,1,0:T(8,128)(2,1)} %param.5), kind=kLoop, calls=%fused_computation.3 | loop fusion | bytes 786432 | tf_op jit(solution)/shard_map/slice | solution.py:162
  1.2 0.2 pad_maximum_fusion
  1.5 0.7 collective-permute-start.2
  2.2 19.1 %collective-permute-start.1 = (bf16[24,64,128]{2,1,0:T(8,128)(2,1)S(1)}, bf16[24,64,128]{2,1,0:T(8,128)(2,1)S(1)}, u32[]{:S(2)}, u32[]{:S(2)}) collective-permute-start(bf16[24,64,128]{2,1,0:T(8,128)(2,1)S(1)} %pad_maximum_fusion), channel_id=1, source_target_pairs={{16,32},{32,16},{48,64},{64,48},{80,96},{96,80},{112,128},{128,112... | collective-permute-start | bytes 1179656 | tf_op jit(solution)/shard_map/ppermute | solution.py:164
  21.3 1.9 %collective-permute-start = (bf16[24,64,128]{2,1,0:T(8,128)(2,1)S(1)}, bf16[24,64,128]{2,1,0:T(8,128)(2,1)S(1)}, u32[]{:S(2)}, u32[]{:S(2)}) collective-permute-start(bf16[24,64,128]{2,1,0:T(8,128)(2,1)S(1)} %pad_maximum_fusion), channel_id=1, source_target_pairs={{0,16},{16,0},{128,144},{144,128},{256,272},{272,256},{384,400},{4... | collective-permute-start | bytes 1179656 | tf_op jit(solution)/shard_map/ppermute | solution.py:163
  23.2 0.0 copy-done.1
  23.3 0.0 copy-start
  23.3 2.8 %copy-done = bf16[1,48,8,64,64]{4,3,2,1,0:T(8,128)(2,1)S(1)} copy-done((bf16[1,48,8,64,64]{4,3,2,1,0:T(8,128)(2,1)S(1)}, bf16[1,48,8,64,64]{4,3,2,1,0:T(8,128)(2,1)}, u32[]{:S(2)}) %copy-start) | copy-done | bytes 3145752
  26.0 0.0 copy-start.2
  26.0 0.0 copy-start.3
  26.0 2.8 %project.1 = (bf16[48,8,64,64]{3,2,1,0:T(8,128)(2,1)S(1)}, bf16[144,64,128]{2,1,0:T(8,128)(2,1)S(1)}, f32[12288,128]{1,0:T(8,128)S(1)}) custom-call(bf16[48,64,64]{2,1,0:T(8,128)(2,1)S(1)} %bitcast.19, bf16[48,8,64,64]{3,2,1,0:T(8,128)(2,1)S(1)} %bitcast.18), custom_call_target="tpu_custom_call" | custom-call | flops 1610612736 | bytes 6291456 | tf_op jit(solution)/shard_map/project/pallas_call | solution.py:173
  28.9 0.0 collective-permute-done.2.late_ref
  28.9 1.2 %collective-permute-done.1.cross_ref = bf16[24,64,128]{2,1,0:T(8,128)(2,1)S(1)} collective-permute-done((bf16[24,64,128]{2,1,0:T(8,128)(2,1)S(1)}, bf16[24,64,128]{2,1,0:T(8,128)(2,1)S(1)}, u32[]{:S(2)}, u32[]{:S(2)}) %collective-permute-start.1) | collective-permute-done | bytes 393248 | tf_op jit(solution)/shard_map/ppermute | solution.py:164
  30.1 2.8 %collective-permute-done.early_ref = bf16[24,64,128]{2,1,0:T(8,128)(2,1)S(1)} collective-permute-done((bf16[24,64,128]{2,1,0:T(8,128)(2,1)S(1)}, bf16[24,64,128]{2,1,0:T(8,128)(2,1)S(1)}, u32[]{:S(2)}, u32[]{:S(2)}) %collective-permute-start) | collective-permute-done | bytes 393248 | tf_op jit(solution)/shard_map/ppermute | solution.py:163
  32.9 0.0 copy-done.2
  32.9 0.0 copy-done.3
  32.9 4.7 %galerkin.1 = (f32[8,384,128]{2,1,0:T(8,128)S(1)}, bf16[8,384,128]{2,1,0:T(8,128)(2,1)S(1)}, bf16[144,64,128]{2,1,0:T(8,128)(2,1)S(1)}, f32[12288,128]{1,0:T(8,128)S(1)}) custom-call(s32[8,48]{1,0:T(8,128)S(1)} %bitcast.20, s32[8,48]{1,0:T(8,128)S(1)} %bitcast.21, ...), custom_call_target="tpu_custom_call", output_to_operand_aliasing={{2}: (6, {}), {3}: (7, {})} | custom-call | tf_op jit(solution)/shard_map/galerkin/pallas_call | solution.py:186
  37.7 3.7 %collective-permute-start.3 = (bf16[8,384,128]{2,1,0:T(8,128)(2,1)S(1)}, bf16[8,384,128]{2,1,0:T(8,128)(2,1)S(1)}, u32[]{:S(2)}, u32[]{:S(2)}) collective-permute-start(bf16[8,384,128]{2,1,0:T(8,128)(2,1)S(1)} %get-tuple-element.14), channel_id=1, source_target_pairs={{0,1},{1,0},{2,3},{3,2},{4,5},{5,4},{6,7},{7,6},{8,9},{9,8},{10,11... | collective-permute-start | bytes 2359304 | tf_op jit(solution)/shard_map/ppermute | solution.py:201
  41.4 1.9 %collective-permute-done.3 = bf16[8,384,128]{2,1,0:T(8,128)(2,1)S(1)} collective-permute-done((bf16[8,384,128]{2,1,0:T(8,128)(2,1)S(1)}, bf16[8,384,128]{2,1,0:T(8,128)(2,1)S(1)}, u32[]{:S(2)}, u32[]{:S(2)}) %collective-permute-start.3) | collective-permute-done | bytes 786464 | tf_op jit(solution)/shard_map/ppermute | solution.py:201
  43.3 0.2 add_convert_fusion
  43.5 29.4 %all_to_all.10.got_ref = bf16[8,384,128]{2,1,0:T(8,128)(2,1)S(1)} all-to-all(bf16[8,384,128]{2,1,0:T(8,128)(2,1)S(1)} %add_convert_fusion), channel_id=1, replica_groups={{0,2,4,6,8,10,12,14},{1,3,5,7,9,11,13,15},{16,18,20,22,24,26,28,30},{17..., dimensions={0} | all-to-all | bytes 1572864 | tf_op jit(solution)/shard_map/all_to_all | solution.py:206
  72.9 0.4 finish.1
  73.2 23.1 %all_to_all.11.mine = bf16[8,384,128]{2,1,0:T(8,128)(2,1)S(1)} all-to-all(bf16[8,384,128]{2,1,0:T(8,128)(2,1)S(1)} %finish.1), channel_id=1, replica_groups={{0,2,4,6,8,10,12,14},{1,3,5,7,9,11,13,15},{16,18,20,22,24,26,28,30},{17..., dimensions={0} | all-to-all | bytes 1572864 | tf_op jit(solution)/shard_map/all_to_all | solution.py:216
  96.4 5.2 %collective-permute-start.4 = (bf16[8,384,128]{2,1,0:T(8,128)(2,1)S(1)}, bf16[8,384,128]{2,1,0:T(8,128)(2,1)S(1)}, u32[]{:S(2)}, u32[]{:S(2)}) collective-permute-start(bf16[8,384,128]{2,1,0:T(8,128)(2,1)S(1)} %all_to_all.11.mine), channel_id=1, source_target_pairs={{0,1},{1,0},{2,3},{3,2},{4,5},{5,4},{6,7},{7,6},{8,9},{9,8},{10,11... | collective-permute-start | bytes 2359304 | tf_op jit(solution)/shard_map/ppermute | solution.py:217
  101.6 1.9 %collective-permute-done.4.other = bf16[8,384,128]{2,1,0:T(8,128)(2,1)S(1)} collective-permute-done((bf16[8,384,128]{2,1,0:T(8,128)(2,1)S(1)}, bf16[8,384,128]{2,1,0:T(8,128)(2,1)S(1)}, u32[]{:S(2)}, u32[]{:S(2)}) %collective-permute-start.4) | collective-permute-done | bytes 786464 | tf_op jit(solution)/shard_map/ppermute | solution.py:217
  103.5 1.5 %spread.1 = bf16[4096,192]{1,0:T(8,128)(2,1)} custom-call(s32[1]{0:T(128)S(6)} %select_n.7.first, s32[1]{0:T(128)S(6)} %and.10.second, bf16[8,384,128]{2,1,0:T(8,128)(2,1)S(1)} %all_to_all.11.mine, bf16[8,384,128]{2,1,0:T(8,128)(2,1)S(1)} %collective-permute-done.4.other), custom_call_target="tpu_custom_call" | custom-call | tf_op jit(solution)/shard_map/spread/pallas_call | solution.py:218
Async XLA Ops:
  0.0 23.2 %copy-start.1 = (bf16[1,48,64,64]{3,2,1,0:T(8,128)(2,1)S(1)}, bf16[1,48,64,64]{3,2,1,0:T(8,128)(2,1)}, u32[]{:S(2)}) copy-start(bf16[1,48,64,64]{3,2,1,0:T(8,128)(2,1)} %param.5) | copy-start | bytes 1179652
  1.5 27.4 %collective-permute-start.2 = (bf16[24,64,128]{2,1,0:T(8,128)(2,1)S(1)}, bf16[24,64,128]{2,1,0:T(8,128)(2,1)S(1)}, u32[]{:S(2)}, u32[]{:S(2)}) collective-permute-start(bf16[24,64,128]{2,1,0:T(8,128)(2,1)S(1)} %pad_maximum_fusion), channel_id=1, source_target_pairs={{32,48},{48,32},{64,80},{80,64},{96,112},{112,96},{160,176},{176,1... | collective-permute-start | bytes 1179656 | tf_op jit(solution)/shard_map/ppermute | solution.py:165
  2.2 28.0 %collective-permute-start.1 = (bf16[24,64,128]{2,1,0:T(8,128)(2,1)S(1)}, bf16[24,64,128]{2,1,0:T(8,128)(2,1)S(1)}, u32[]{:S(2)}, u32[]{:S(2)}) collective-permute-start(bf16[24,64,128]{2,1,0:T(8,128)(2,1)S(1)} %pad_maximum_fusion), channel_id=1, source_target_pairs={{16,32},{32,16},{48,64},{64,48},{80,96},{96,80},{112,128},{128,112... | collective-permute-start | bytes 1179656 | tf_op jit(solution)/shard_map/ppermute | solution.py:164
  21.3 11.6 %collective-permute-start = (bf16[24,64,128]{2,1,0:T(8,128)(2,1)S(1)}, bf16[24,64,128]{2,1,0:T(8,128)(2,1)S(1)}, u32[]{:S(2)}, u32[]{:S(2)}) collective-permute-start(bf16[24,64,128]{2,1,0:T(8,128)(2,1)S(1)} %pad_maximum_fusion), channel_id=1, source_target_pairs={{0,16},{16,0},{128,144},{144,128},{256,272},{272,256},{384,400},{4... | collective-permute-start | bytes 1179656 | tf_op jit(solution)/shard_map/ppermute | solution.py:163
  23.3 2.8 %copy-start = (bf16[1,48,8,64,64]{4,3,2,1,0:T(8,128)(2,1)S(1)}, bf16[1,48,8,64,64]{4,3,2,1,0:T(8,128)(2,1)}, u32[]{:S(2)}) copy-start(bf16[1,48,8,64,64]{4,3,2,1,0:T(8,128)(2,1)} %param.4) | copy-start | bytes 9437188
  26.0 6.9 %copy-start.2 = (s32[1,48,8]{1,2,0:T(8,128)S(1)}, s32[1,48,8]{1,2,0:T(8,128)}, u32[]{:S(2)}) copy-start(s32[1,48,8]{1,2,0:T(8,128)} %param.6) | copy-start | bytes 4612
  26.0 6.9 %copy-start.3 = (s32[1,48,8]{1,2,0:T(8,128)S(1)}, s32[1,48,8]{1,2,0:T(8,128)}, u32[]{:S(2)}) copy-start(s32[1,48,8]{1,2,0:T(8,128)} %param.7) | copy-start | bytes 4612
  37.7 5.6 %collective-permute-start.3 = (bf16[8,384,128]{2,1,0:T(8,128)(2,1)S(1)}, bf16[8,384,128]{2,1,0:T(8,128)(2,1)S(1)}, u32[]{:S(2)}, u32[]{:S(2)}) collective-permute-start(bf16[8,384,128]{2,1,0:T(8,128)(2,1)S(1)} %get-tuple-element.14), channel_id=1, source_target_pairs={{0,1},{1,0},{2,3},{3,2},{4,5},{5,4},{6,7},{7,6},{8,9},{9,8},{10,11... | collective-permute-start | bytes 2359304 | tf_op jit(solution)/shard_map/ppermute | solution.py:201
  96.4 7.1 %collective-permute-start.4 = (bf16[8,384,128]{2,1,0:T(8,128)(2,1)S(1)}, bf16[8,384,128]{2,1,0:T(8,128)(2,1)S(1)}, u32[]{:S(2)}, u32[]{:S(2)}) collective-permute-start(bf16[8,384,128]{2,1,0:T(8,128)(2,1)S(1)} %all_to_all.11.mine), channel_id=1, source_target_pairs={{0,1},{1,0},{2,3},{3,2},{4,5},{5,4},{6,7},{7,6},{8,9},{9,8},{10,11... | collective-permute-start | bytes 2359304 | tf_op jit(solution)/shard_map/ppermute | solution.py:217
